TPU v7x, 32 devices: a whole 2x2x4 slice. The times are simulated.
32 devices in a mesh: row: 2 (over y), col: 4 (over x, core), tm: 4 (over z).
Axes of the slice: x: 2, y: 2, z: 4, core: 2. Of those that a mesh axis runs over, the one named last changes fastest.
Arguments:
- filled_orbitals: bfloat16 [4, 1024, 1024], P('col', 'row', 'tm'), may hold values from -0.1875 to 0.1875
- empty_orbitals: bfloat16 [4, 1024, 3072], P('col', 'row', 'tm'), may hold values from -0.109375 to 0.109375
- filled_depth: bfloat16 [1024], P('tm'), may hold values from 0.019897461 to 2
- empty_depth: bfloat16 [3072], P('tm'), may hold values from 0.019897461 to 2
- time_points: float32 [4], P('tm'), may hold values from 0.05 to 8
- cosine_weights: float32 [4, 4], replicated, may hold values from -3 to 3
Outputs:
- polar_freq: float32 [4, 4, 1024, 4096], P(None, None, ('row', 'tm'), 'col')
All inputs are finite; a program needn't handle non-finite values.
Results may differ from a plain program's by a relative error of at most 0.0033.
Values may be sent and summed in bfloat16 or wider, within the bound.
No kernel may reach another device: no remote copies, remote signals or barrier semaphores. Data moves between devices by JAX's collectives and lax.ppermute only.
A program may use at most 128 MiB of HBM per device.

v0:
```python
import jax
import jax.numpy as jnp
from jax import lax
from jax.sharding import PartitionSpec as P


def tile_product(left_points, right_points, depths, tau_value):
    band_count = left_points.shape[-1]
    weight_row = jnp.exp(-depths.astype(jnp.float32) * tau_value)
    scaled = (
        right_points.reshape(-1, band_count).astype(jnp.float32) * weight_row[None, :]
    ).astype(jnp.bfloat16)
    return lax.dot_general(
        left_points.reshape(-1, band_count),
        scaled,
        (((1,), (1,)), ((), ())),
        preferred_element_type=jnp.float32,
    )


def on_device(
    filled_orbitals, empty_orbitals, filled_depth, empty_depth, time_points, cosine_weights
):
    tau_value = time_points[0]
    filled_bands, empty_bands, filled_all, empty_all = (
        lax.all_gather(filled_orbitals, "tm", axis=2, tiled=True),
        lax.all_gather(empty_orbitals, "tm", axis=2, tiled=True),
        lax.all_gather(filled_depth, "tm", axis=0, tiled=True),
        lax.all_gather(empty_depth, "tm", axis=0, tiled=True),
    )
    filled_rows, empty_rows = (
        lax.all_gather(filled_bands, "col", axis=0, tiled=True),
        lax.all_gather(empty_bands, "col", axis=0, tiled=True),
    )
    column_filled, column_empty = lax.all_gather(
        (filled_bands, empty_bands), "row", axis=1, tiled=True
    )
    green_filled = tile_product(filled_rows, column_filled, filled_all, tau_value)
    green_empty = tile_product(empty_rows, column_empty, empty_all, tau_value)
    polar_time = (
        (-(green_filled * green_empty))
        .astype(jnp.bfloat16)
        .reshape(filled_rows.shape[0], filled_rows.shape[1], -1)
    )
    return jnp.einsum(
        "ft,tabc->fabc",
        cosine_weights,
        lax.all_to_all(polar_time[None], "tm", split_axis=2, concat_axis=0, tiled=True).astype(
            jnp.float32
        ),
        precision=lax.Precision.HIGHEST,
    )


def solution(mesh):
    in_specs = (P("col", "row", "tm"), P("col", "row", "tm"), P("tm"), P("tm"), P("tm"), P())
    out_specs = P(None, None, ("row", "tm"), "col")
    return jax.shard_map(
        on_device, mesh=mesh, in_specs=in_specs, out_specs=out_specs, check_vma=False
    )
```

profile of v0, /device:TPU:0, one launch (start us, length us, event | category | flops | bytes accessed | tf_op | source)
XLA Modules:
  0.0 491.7 jit_solution(13205183618008928850)
XLA Ops:
  6.5 0.0 copy-start
  6.5 0.0 all-gather.15.cloned.1.call-start
  6.5 0.7 all-gather.15.cloned.1.call-update
  7.3 0.0 all-gather.9.cloned.1.call-start
  7.3 0.7 all-gather.9.cloned.1.call-update
  8.0 0.0 all-gather.17.cloned.1.call-start
  8.1 67.0 %all-gather.15.cloned.1.call-done = bf16[1,512,3072]{2,1,0:T(8,128)(2,1)} async-done(((bf16[1,512,768]{2,1,0:T(8,128)(2,1)}), bf16[1,512,3072]{2,1,0:T(8,128)(2,1)}) %all-gather.15.cloned.1.call-update) | async-done | bytes 3145744 | tf_op jit(solution)/shard_map/all_gather | solution.py:27
  75.1 0.0 copy-start.1
  75.1 0.0 all-gather.17.cloned.1.call-update
  75.1 0.0 all-gather.19.cloned.1.call-start
  75.2 0.5 all-gather.19.cloned.1.call-update
  75.7 0.0 all-gather.11.cloned.1.call-start
  75.8 29.5 %all-gather.9.cloned.1.call-done = bf16[1,512,1024]{2,1,0:T(8,128)(2,1)} async-done(((bf16[1,512,256]{2,1,0:T(8,128)(2,1)}), bf16[1,512,1024]{2,1,0:T(8,128)(2,1)}) %all-gather.9.cloned.1.call-update) | async-done | bytes 1048592 | tf_op jit(solution)/shard_map/all_gather | solution.py:26
  105.3 0.0 all-gather.11.cloned.1.call-update
  105.3 0.0 all-gather.13.cloned.1.call-start
  105.3 0.5 all-gather.13.cloned.1.call-update
  106.5 0.0 copy-done.1
  106.5 0.0 copy-done.2
  106.6 10.1 %all-gather = bf16[4,1,256]{2,1,0:T(2,128)(2,1)S(1)} all-gather(bf16[1,1,256]{2,1,0:T(2,128)(2,1)S(1)} %reshape.26), channel_id=1, replica_groups=mesh['row'=2,'col'=4,'tm'=4] {'tm'}, dimensions={0}, use_global_device_ids=true | all-gather | bytes 2560 | tf_op jit(solution)/shard_map/all_gather | solution.py:28
  116.7 13.1 %all-gather.1 = bf16[4,1,768]{2,1,0:T(2,128)(2,1)S(1)} all-gather(bf16[1,1,768]{2,1,0:T(2,128)(2,1)S(1)} %reshape.28), channel_id=1, replica_groups=mesh['row'=2,'col'=4,'tm'=4] {'tm'}, dimensions={0}, use_global_device_ids=true | all-gather | bytes 7680 | tf_op jit(solution)/shard_map/all_gather | solution.py:29
  129.8 55.7 %all-gather.17.cloned.1.call-done = bf16[1,1024,3072]{2,1,0:T(8,128)(2,1)} async-done(((bf16[1,512,3072]{2,1,0:T(8,128)(2,1)}), bf16[1,1024,3072]{2,1,0:T(8,128)(2,1)}) %all-gather.17.cloned.1.call-update) | async-done | bytes 6291472 | tf_op jit(solution)/shard_map/all_gather | solution.py:35
  185.5 83.5 %all-gather.19.cloned.1.call-done = bf16[4,512,3072]{2,1,0:T(8,128)(2,1)} async-done(((bf16[1,512,3072]{2,1,0:T(8,128)(2,1)}), bf16[4,512,3072]{2,1,0:T(8,128)(2,1)}) %all-gather.19.cloned.1.call-update) | async-done | bytes 12582928 | tf_op jit(solution)/shard_map/all_gather | solution.py:33
  269.0 18.9 %fusion.1 = f32[1024,2048]{1,0:T(8,128)} fusion(bf16[2048,3072]{1,0:T(8,128)(2,1)} %bitcast.35, bf16[1,1024,3072]{2,1,0:T(8,128)(2,1)} %all-gather.17.cloned.1.call-done, f32[3072]{0:T(1024)S(1)} %bitcast.33), kind=kOutput, calls=%fused_computation.3 | convolution fusion | flops 12894339072 | bytes 27275264 | tf_op jit(solution)/shard_map/dot_general | solution.py:13
  287.9 15.6 %all-gather.11.cloned.1.call-done = bf16[1,1024,1024]{2,1,0:T(8,128)(2,1)} async-done(((bf16[1,512,1024]{2,1,0:T(8,128)(2,1)}), bf16[1,1024,1024]{2,1,0:T(8,128)(2,1)}) %all-gather.11.cloned.1.call-update) | async-done | bytes 2097168 | tf_op jit(solution)/shard_map/all_gather | solution.py:35
  303.5 35.9 %all-gather.13.cloned.1.call-done = bf16[4,512,1024]{2,1,0:T(8,128)(2,1)} async-done(((bf16[1,512,1024]{2,1,0:T(8,128)(2,1)}), bf16[4,512,1024]{2,1,0:T(8,128)(2,1)}) %all-gather.13.cloned.1.call-update) | async-done | bytes 4194320 | tf_op jit(solution)/shard_map/all_gather | solution.py:32
  339.4 11.8 %fusion.6 = bf16[2048,1024]{0,1:T(8,128)(2,1)} fusion(f32[1024,2048]{1,0:T(8,128)} %fusion.1, bf16[2048,1024]{1,0:T(8,128)(2,1)} %bitcast.36, bf16[1,1024,1024]{2,1,0:T(8,128)(2,1)} %all-gather.11.cloned.1.call-done, f32[1024]{0:T(1024)S(1)} %bitcast.34), kind=kOutput, calls=%fused_computation.9 | convolution fusion | flops 4304404480 | bytes 18878464 | tf_op jit(solution)/shard_map/dot_general | solution.py:13
  351.2 7.8 %broadcast_in_dim_reshape.3 = bf16[1,4,512,1024]{2,1,3,0:T(4,128)(2,1)} reshape(bf16[2048,1024]{0,1:T(8,128)(2,1)} %fusion.6) | data formatting | bytes 8388608 | tf_op jit(solution)/shard_map/broadcast_in_dim;reshape | solution.py:48
  359.0 10.0 %copy.11 = bf16[1,4,512,1024]{3,1,0,2:T(4,128)(2,1)} copy(bf16[1,4,512,1024]{2,1,3,0:T(4,128)(2,1)} %broadcast_in_dim_reshape.3) | data formatting | bytes 8388608 | tf_op jit(solution)/shard_map/broadcast_in_dim;reshape | solution.py:48
  369.0 98.1 %all_to_all.18 = bf16[1,4,512,1024]{3,1,0,2:T(4,128)(2,1)S(1)} all-to-all(bf16[1,4,512,1024]{3,1,0,2:T(4,128)(2,1)} %copy.11), channel_id=1, replica_groups=mesh['row'=2,'col'=4,'tm'=4] {'tm'}, dimensions={2} | all-to-all | bytes 8388608 | tf_op jit(solution)/shard_map/all_to_all | solution.py:48
  467.2 0.0 copy-done
  467.2 9.4 %convolution_bitcast_fusion = f32[4,4,128,1024]{3,0,2,1:T(4,128)S(1)} fusion(bf16[1,4,4,128,1024]{4,1,3,2,0:T(4,128)(2,1)S(1)} %bitcast.32, f32[4,4]{1,0:T(4,128)S(1)} %copy-done), kind=kOutput, calls=%fused_computation.5 | convolution fusion | flops 100663296 | bytes 12582976 | tf_op jit(solution)/shard_map/ft,tabc->fabc/dot_general | solution.py:45
  476.6 8.3 %copy.14 = f32[4,4,128,1024]{3,2,1,0:T(8,128)} copy(f32[4,4,128,1024]{3,0,2,1:T(4,128)S(1)} %convolution_bitcast_fusion) | data formatting | bytes 16777216 | tf_op jit(solution)/shard_map/ft,tabc->fabc/dot_general | solution.py:45
  (5 shorter events, 0.1 us)
Async XLA Ops:
  6.5 460.6 %copy-start = (f32[4,4]{1,0:T(4,128)S(1)}, f32[4,4]{1,0:T(4,128)}, u32[]{:S(2)}) copy-start(f32[4,4]{1,0:T(4,128)} %param.11) | copy-start | bytes 196
  6.5 68.6 %all-gather.15.cloned.1.call-start = ((), (), s32[]{:S(2)}) async-start(), calls=%async_computation.4 | async-start | bytes 3932160 | tf_op jit(solution)/shard_map/all_gather | solution.py:27
  7.3 98.0 %all-gather.9.cloned.1.call-start = ((), (), s32[]{:S(2)}) async-start(), calls=%async_computation.1 | async-start | bytes 1310720 | tf_op jit(solution)/shard_map/all_gather | solution.py:26
  8.0 177.5 %all-gather.17.cloned.1.call-start = ((), (), s32[]{:S(2)}) async-start(), calls=%async_computation.5 | async-start | bytes 9437184 | tf_op jit(solution)/shard_map/all_gather | solution.py:35
  75.1 31.4 %copy-start.1 = (bf16[768]{0:T(1024)(128)(2,1)S(1)}, bf16[768]{0:T(1024)(128)(2,1)}, u32[]{:S(2)}) copy-start(bf16[768]{0:T(1024)(128)(2,1)} %param.9) | copy-start | bytes 4612
  75.1 31.4 %copy-start.2 = (bf16[256]{0:T(256)(128)(2,1)S(1)}, bf16[256]{0:T(256)(128)(2,1)}, u32[]{:S(2)}) copy-start(bf16[256]{0:T(256)(128)(2,1)} %param.8) | copy-start | bytes 1540
  75.1 193.9 %all-gather.19.cloned.1.call-start = ((), (), s32[]{:S(2)}) async-start(), calls=%async_computation.6 | async-start | bytes 15728640 | tf_op jit(solution)/shard_map/all_gather | solution.py:33
  75.7 227.8 %all-gather.11.cloned.1.call-start = ((), (), s32[]{:S(2)}) async-start(), calls=%async_computation.2 | async-start | bytes 3145728 | tf_op jit(solution)/shard_map/all_gather | solution.py:35
  105.3 234.2 %all-gather.13.cloned.1.call-start = ((), (), s32[]{:S(2)}) async-start(), calls=%async_computation.3 | async-start | bytes 5242880 | tf_op jit(solution)/shard_map/all_gather | solution.py:32
Sparse Core Ops, SparseCore 0:
  8.9 66.1 all-gather.14
  76.7 28.5 all-gather.8
  106.8 78.6 all-gather.16
  186.9 82.0 all-gather.18
  270.4 33.0 all-gather.10
  305.0 34.4 all-gather.12
where the time goes:
time: 492 us
  waiting for transfers between devices  290 us (59%)
  blocking collectives  121 us (25%)
  matrix products  40.1 us (8%)
  local copies, waits for them, and re-layouts  26.1 us (5%)
  between operations  14.2 us (3%)
    all_to_all x1, blocking collectives, on_device(): lax.all_to_all(polar_time[None], 'tm', split_axis=2, concat_axis=0, tiled...  98.1 us
    all_gather x1, waiting for transfers between devices, on_device(): lax.all_gather(empty_bands, 'col', axis=0, tiled=True)  83.5 us
    all_gather x2, waiting for transfers between devices, on_device(): lax.all_gather((filled_bands, empty_bands), 'row', axis=1, tiled=True)  71.3 us
    all_gather x1, waiting for transfers between devices, on_device(): lax.all_gather(empty_orbitals, 'tm', axis=2, tiled=True)  67 us
    all_gather x1, waiting for transfers between devices, on_device(): lax.all_gather(filled_bands, 'col', axis=0, tiled=True)  35.9 us
    dot_general x2, matrix products, tile_product(): lax.dot_general(left_points.reshape(-1, band_count), scaled, (((1,), (1,)...  30.6 us
    all_gather x1, waiting for transfers between devices, on_device(): lax.all_gather(filled_orbitals, 'tm', axis=2, tiled=True)  29.5 us
    another operation x2, local copies, waits for them, and re-layouts, on_device(): polar_time[None]  17.8 us
  transfers between devices with their start and end apart: 6, of which 6 were waited for; matrix products, arithmetic and copies ran while one was open for 4% of the time, Pallas kernels for 0%

commit v1 on v0

v1 whole, which is shorter than its diff:
```python
import functools

import jax
import jax.numpy as jnp
from jax import lax
from jax.experimental import pallas as pl
from jax.experimental.pallas import tpu as pltpu
from jax.sharding import PartitionSpec as P


LANES = 128


def make_plan(n, rows, cols):
    plan, known = [], set()

    def emit(axis, shift, source, target, half=None):
        if target not in known:
            known.add(target)
            plan.append(("move", axis, shift, source, target, half))

    def own(m, k):
        if k == 0:
            known.add(("P", m, 0))
        elif m == 0 or k in (1, n - 1):
            emit("tm", k if k <= n // 2 else k - n, ("S", (k + m) % n), ("P", m, k))
        elif 2 * k == n and 2 * m == n:
            own(m - 1, k + 1)
            own(m + 1, k - 1)
            emit("tm", -1, ("P", m - 1, k + 1), ("P", m, k, 0), 0)
            emit("tm", 1, ("P", (m + 1) % n, k - 1), ("P", m, k, 1), 1)
        elif 2 * k < n or (2 * k == n and 2 * m > n):
            own((m + 1) % n, k - 1)
            emit("tm", 1, ("P", (m + 1) % n, k - 1), ("P", m, k))
        else:
            own(m - 1, k + 1)
            emit("tm", -1, ("P", m - 1, k + 1), ("P", m, k))

    def parts(m, k):
        return [(m, k, 0), (m, k, 1)] if k and 2 * k == n and 2 * m == n else [(m, k)]

    def across(m, k):
        for dy in range(1, rows):
            for part in parts(m, k):
                emit("row", dy, ("P", *part), ("Y", dy, *part))

    def column(d, k):
        if d:
            low = d & 1
            if low and d > 1:
                emit("col", low, ("F", d - low, k), ("F", d, k))
            else:
                emit("col", d, ("P", 0, k), ("F", d, k))

    def kernel(m, dy):
        plan.append(("kernel", m, dy))

    near = sorted(range(1, n), key=lambda k: (min(k, n - k), k))
    late = [m for pair in zip(range(1, n), range(n - 1, 0, -1)) for m in pair]
    late = list(dict.fromkeys(late))
    for k in near:
        own(0, k)
    across(0, 0)
    for d in range(2, cols, 2):
        column(d, 0)
    for k in near:
        plan.append(("move", "tm", k, ("D", 0), ("D", k), None))
    for m in late[:1]:
        for k in (1, n - 1):
            own(m, k)
    for m in late:
        across(m, 0)
    column(1, 0)
    for k in near:
        for d in range(2, cols, 2):
            column(d, k)
        across(0, k)
        if min(k, n - k) == 1 and 2 * k > n:
            for m in late[:2]:
                for j in near:
                    own(m, j)
        column(1, k)
    for m in late:
        for k in (1, n - 1):
            own(m, k)
    for k in [0, *near]:
        for d in range(3, cols, 2):
            column(d, k)
    kernel(0, 0)
    done = [(0, dy) for dy in range(1, rows)]
    ready = []
    for m in late:
        for k in near:
            own(m, k)
        for k in near:
            across(m, k)
        for item in done:
            kernel(*item)
        kernel(m, 0)
        done = ready
        ready = [(m, dy) for dy in range(1, rows)]
    for item in [*done, *ready]:
        kernel(*item)
    return plan


def chunk_kernel(cuts, count, assemble, *refs):
    refs = list(refs)
    place, cosines, scale_o, scale_e = refs[:4]
    pieces = refs[4 : 4 + len(cuts)]
    rest = refs[4 + len(cuts) :]
    freqs, times = cosines.shape
    if assemble:
        blocks, rest = rest[: assemble * count], rest[assemble * count :]
        out, keep_o, keep_e = rest[:3]
        rest = rest[3:]
    else:
        kept_o, kept_e, _, out = rest[:4]
        rest = rest[4:]
    fo, fe, co, ce, so, se, go, ge, ob, piece_sem, first_sem, out_sem = rest
    bo, be = co.shape[1] // count, ce.shape[1] // count
    width = co.shape[0]

    def pair(source, start, size, at, into_o, into_e, sem, i):
        rows = pl.ds(start, size)
        return [
            pltpu.make_async_copy(
                source.at[:, pl.ds(0, bo)],
                into_o.at[rows, pl.ds(at * bo, bo)],
                sem.at[2 * i],
            ),
            pltpu.make_async_copy(
                source.at[:, pl.ds(bo, be)],
                into_e.at[rows, pl.ds(at * be, be)],
                sem.at[2 * i + 1],
            ),
        ]

    loads = []
    for i, (ref, (start, size, at)) in enumerate(zip(pieces, cuts)):
        loads += pair(ref, start, size, at, co, ce, piece_sem, i)
    if assemble:
        firsts = []
        for i, ref in enumerate(blocks):
            d, k = divmod(i, count)
            firsts += pair(ref, d * width, width, k, fo, fe, first_sem, i)
    else:
        firsts = [
            pltpu.make_async_copy(kept_o, fo, first_sem.at[0]),
            pltpu.make_async_copy(kept_e, fe, first_sem.at[1]),
        ]
    for copy in loads + firsts:
        copy.start()
    for copy in loads:
        copy.wait()

    step = 16

    @pl.loop(0, width // step)
    def _(i):
        rows = pl.ds(pl.multiple_of(i * step, step), step)
        for source, scale, into in ((co, scale_o, so), (ce, scale_e, se)):
            wide = source[rows, :].astype(jnp.float32)
            for t in range(times):
                at = pl.ds(pl.multiple_of(t * width + i * step, step), step)
                into[at, :] = (wide * scale[t : t + 1, :]).astype(jnp.bfloat16)

    for copy in firsts:
        copy.wait()
    keeps = []
    if assemble:
        keeps = [
            pltpu.make_async_copy(fo, keep_o, out_sem.at[1]),
            pltpu.make_async_copy(fe, keep_e, out_sem.at[2]),
        ]
        for copy in keeps:
            copy.start()
    contract = (((1,), (1,)), ((), ()))
    go[...] = lax.dot_general(fo[...], so[...], contract, preferred_element_type=jnp.float32)
    ge[...] = lax.dot_general(fe[...], se[...], contract, preferred_element_type=jnp.float32)

    column, z = place[0], place[2]
    weights = [
        [cosines[f, lax.rem(z + times - t, times)] for t in range(times)] for f in range(freqs)
    ]
    tall = 32
    for d in range(fo.shape[0] // width):
        q = jnp.bitwise_xor(column, d)

        @pl.loop(0, width // tall)
        def _(i, d=d, q=q):
            rows = pl.ds(pl.multiple_of(d * width + i * tall, tall), tall)
            into = pl.ds(pl.multiple_of(i * tall, tall), tall)
            totals = [None] * freqs
            for t in range(times):
                lanes = pl.ds(t * width, width)
                polar = (-(go[rows, lanes] * ge[rows, lanes])).astype(jnp.bfloat16)
                polar = polar.astype(jnp.float32)
                for f in range(freqs):
                    term = weights[f][t] * polar
                    totals[f] = term if t == 0 else totals[f] + term
            for f in range(freqs):
                ob[f, q, into, :] = totals[f]

    put = pltpu.make_async_copy(
        ob,
        out.at[:, :, :, pl.ds(pl.multiple_of(place[1] * width, width), width)],
        out_sem.at[0],
    )
    put.start()
    for copy in [*keeps, put]:
        copy.wait()


def chunk_call(place, cosines, scales, pieces, cuts, firsts, out, shape, count):
    width = sum(size for _, size, at in cuts if at == 0)
    freqs, cols, _, _ = shape
    times = cosines.shape[1]
    ko, ke = scales[0].shape[1], scales[1].shape[1]
    assemble = cols if isinstance(firsts, list) else 0
    tile = cols * width
    hbm = pl.BlockSpec(memory_space=pl.ANY)
    smem = pl.BlockSpec(memory_space=pltpu.SMEM)
    vmem = pl.BlockSpec(memory_space=pltpu.VMEM)
    result = jax.ShapeDtypeStruct(shape, jnp.float32)
    operands = [place, cosines, *scales, *pieces]
    in_specs = [smem, smem, vmem, vmem] + [hbm] * len(pieces)
    if assemble:
        operands += firsts
        in_specs += [hbm] * len(firsts)
        out_shape = (
            result,
            jax.ShapeDtypeStruct((tile, ko), jnp.bfloat16),
            jax.ShapeDtypeStruct((tile, ke), jnp.bfloat16),
        )
        out_specs = (hbm, hbm, hbm)
        aliases = {}
    else:
        operands += [*firsts, out]
        in_specs += [hbm] * 3
        out_shape, out_specs = result, hbm
        aliases = {len(operands) - 1: 0}
    return pl.pallas_call(
        functools.partial(chunk_kernel, cuts, count, assemble),
        out_shape=out_shape,
        in_specs=in_specs,
        out_specs=out_specs,
        input_output_aliases=aliases,
        scratch_shapes=[
            pltpu.VMEM((tile, ko), jnp.bfloat16),
            pltpu.VMEM((tile, ke), jnp.bfloat16),
            pltpu.VMEM((width, ko), jnp.bfloat16),
            pltpu.VMEM((width, ke), jnp.bfloat16),
            pltpu.VMEM((times * width, ko), jnp.bfloat16),
            pltpu.VMEM((times * width, ke), jnp.bfloat16),
            pltpu.VMEM((tile, times * width), jnp.float32),
            pltpu.VMEM((tile, times * width), jnp.float32),
            pltpu.VMEM((freqs, cols, width, width), jnp.float32),
            pltpu.SemaphoreType.DMA((2 * len(pieces),)),
            pltpu.SemaphoreType.DMA((2 * assemble * count if assemble else 2,)),
            pltpu.SemaphoreType.DMA((3,)),
        ],
        compiler_params=pltpu.CompilerParams(vmem_limit_bytes=40 * 2**20),
        cost_estimate=pl.CostEstimate(
            flops=2 * tile * times * width * (ko + ke),
            bytes_accessed=2 * (tile + width) * (ko + ke) + 4 * freqs * tile * width,
            transcendentals=0,
        ),
        name="chunk",
    )(*operands)


def streamed(plan, sizes, filled, empty, filled_depth, empty_depth, time_points, cosines):
    n, rows, cols = sizes["tm"], sizes["row"], sizes["col"]
    z, r, c = lax.axis_index("tm"), lax.axis_index("row"), lax.axis_index("col")
    points, bo = filled.shape[1:]
    be = empty.shape[2]
    width = points // n
    shape = (cosines.shape[0], cols, width, rows * points)
    whole = jnp.concatenate([filled[0], empty[0]], axis=1)
    values = {}
    for d in range(n):
        own = lax.dynamic_slice_in_dim(whole, lax.rem(z + d, n) * width, width, 0)
        values["S", d] = values["P", d, 0] = own
    depth = jnp.concatenate([filled_depth, empty_depth]).astype(jnp.float32)
    values["D", 0] = jnp.concatenate([depth, jnp.broadcast_to(time_points, (LANES,))])[None, :]
    perms = {
        "tm": lambda s: [(i, (i + s) % n) for i in range(n)],
        "row": lambda s: [(i, (i + s) % rows) for i in range(rows)],
        "col": lambda s: [(i, i ^ s) for i in range(cols)],
    }
    half = width // 2
    scales = firsts = out = None
    for step in plan:
        if step[0] == "move":
            _, axis, shift, source, target, part = step
            value = values[source]
            if part is not None:
                value = value[part * half : (part + 1) * half]
            values[target] = lax.ppermute(value, axis, perms[axis](shift))
            continue
        _, m, dy = step
        if scales is None:
            stacked = jnp.concatenate([values["D", k] for k in range(n)], axis=0)
            deep, tau = stacked[:, :-LANES], stacked[:, bo + be :][:, :1]
            scales = [
                jnp.exp(-piece.reshape(1, -1) * tau) for piece in (deep[:, :bo], deep[:, bo:])
            ]
            firsts = [
                values["F", d, k] if d else values["P", 0, k]
                for d in range(cols)
                for k in range(n)
            ]
        pieces, cuts = [], []
        for k in range(n):
            key = ("Y", dy, m, k) if dy else ("P", m, k)
            if key in values:
                pieces.append(values[key])
                cuts.append((0, width, k))
            else:
                pieces += [values[(*key, h)] for h in (0, 1)]
                cuts += [(0, half, k), (half, half, k)]
        block = lax.rem(r + rows - dy, rows) * n + lax.rem(z + m, n)
        place = jnp.stack([c, block, z]).astype(jnp.int32)
        result = chunk_call(
            place, cosines, scales, pieces, tuple(cuts), firsts, out, shape, n
        )
        if isinstance(firsts, list):
            out, *firsts = result
            firsts = tuple(firsts)
        else:
            out = result
    return out


def gathered(sizes, filled, empty, filled_depth, empty_depth, time_points, cosines):
    points = filled.shape[1]
    width = points // sizes["tm"]
    z = lax.axis_index("tm")

    def green(orbitals, depths):
        mine = lax.all_gather(orbitals[0], "tm", axis=1, tiled=True)
        depths = lax.all_gather(depths, "tm", axis=0, tiled=True).astype(jnp.float32)
        first = lax.all_gather(
            lax.dynamic_slice_in_dim(mine, z * width, width, 0), "col", axis=0, tiled=True
        )
        second = lax.all_gather(mine, "row", axis=0, tiled=True)

        def at(tau):
            scaled = (second.astype(jnp.float32) * jnp.exp(-depths * tau)[None, :]).astype(
                jnp.bfloat16
            )
            return lax.dot_general(
                first, scaled, (((1,), (1,)), ((), ())), preferred_element_type=jnp.float32
            )

        return at

    taus = lax.all_gather(time_points, "tm", axis=0, tiled=True)
    at_o, at_e = green(filled, filled_depth), green(empty, empty_depth)
    total = 0.0
    for t in range(taus.shape[0]):
        polar = (-(at_o(taus[t]) * at_e(taus[t]))).astype(jnp.bfloat16).astype(jnp.float32)
        total = total + cosines[:, t, None, None] * polar[None]
    return total.reshape(cosines.shape[0], sizes["col"], width, -1)


def solution(mesh):
    sizes = dict(mesh.shape)
    in_specs = (P("col", "row", "tm"), P("col", "row", "tm"), P("tm"), P("tm"), P("tm"), P())
    out_specs = P(None, None, ("row", "tm"), "col")
    plan = make_plan(sizes["tm"], sizes["row"], sizes["col"])

    def on_device(filled, *rest):
        width = filled.shape[1] // sizes["tm"]
        if width % LANES or sizes["col"] & (sizes["col"] - 1):
            return gathered(sizes, filled, *rest)
        return streamed(plan, sizes, filled, *rest)

    return jax.shard_map(
        on_device, mesh=mesh, in_specs=in_specs, out_specs=out_specs, check_vma=False
    )
```

time: 492 us -> 163 us (0.33)
  waiting for transfers between devices: 290 us -> 62.6 us
  blocking collectives: 121 us -> 0 us
  Pallas kernels: 0 us -> 47 us
  starting transfers between devices: 0.19 us -> 46.6 us
  matrix products: 40.1 us -> 0 us
  local copies, waits for them, and re-layouts: 26.1 us -> 2.38 us
  between operations: 14.2 us -> 1.09 us
    all_gather x6 -> x0, waiting for transfers between devices: 287 us -> none  [the longest x1 83.5 us: on_device(): lax.all_gather(empty_bands, 'col', axis=0, tiled=True)]
    all_to_all x1 -> x0, blocking collectives: 98.1 us -> none  [on_device(): lax.all_to_all(polar_time[None], 'tm', split_axis=2, concat_axis=0, tiled...]
    ppermute x0 -> x45, waiting for transfers between devices: none -> 62.6 us  [streamed(): values[target] = lax.ppermute(value, axis, perms[axis](shift))]
    pallas_call x0 -> x8, Pallas kernels: none -> 47 us  [chunk_call(): pl.pallas_call(functools.partial(chunk_kernel, cuts, count, assemble), ou...]
    ppermute x0 -> x45, starting transfers between devices: none -> 46.6 us  [streamed(): values[target] = lax.ppermute(value, axis, perms[axis](shift))]
    dot_general x3 -> x0, matrix products: 40.1 us -> none  [the longest x2 30.6 us: tile_product(): lax.dot_general(left_points.reshape(-1, band_count), scaled, (((1,), (1,)...]
    all_gather x2 -> x0, blocking collectives: 23.2 us -> none  [the longest x1 13.1 us: on_device(): lax.all_gather(empty_depth, 'tm', axis=0, tiled=True)]
    another operation x2 -> x0, local copies, waits for them, and re-layouts: 17.8 us -> none  [on_device(): polar_time[None]]
  transfers between devices with their start and end apart: 6 -> 45, of which waited for: 6 -> 13; matrix products, arithmetic and copies ran while one was open for 4% -> 1% of each run, Pallas kernels for 0% -> 25%
where the time goes in v1:
time: 163 us
  waiting for transfers between devices  62.6 us (38%)
  Pallas kernels  47 us (29%)
  starting transfers between devices  46.6 us (29%)
  other arithmetic  2.88 us (2%)
  local copies, waits for them, and re-layouts  2.38 us (1%)
    ppermute x45, waiting for transfers between devices, streamed(): values[target] = lax.ppermute(value, axis, perms[axis](shift))  62.6 us
    pallas_call x8, Pallas kernels, chunk_call(): pl.pallas_call(functools.partial(chunk_kernel, cuts, count, assemble), ou...  47 us
    ppermute x45, starting transfers between devices, streamed(): values[target] = lax.ppermute(value, axis, perms[axis](shift))  46.6 us
  transfers between devices with their start and end apart: 45, of which 13 were waited for; matrix products, arithmetic and copies ran while one was open for 1% of the time, Pallas kernels for 25%

profile of v1, /device:TPU:0, one launch (start us, length us, event | category | flops | bytes accessed | tf_op | source)
XLA Modules:
  0.0 162.6 jit_solution(11301141093052688207)
XLA Ops:
  1.3 3.1 %collective-permute-start.14 = (bf16[128,1024]{1,0:T(8,128)(2,1)S(1)}, bf16[128,1024]{1,0:T(8,128)(2,1)S(1)}, u32[]{:S(2)}, u32[]{:S(2)}) collective-permute-start(bf16[128,1024]{1,0:T(8,128)(2,1)S(1)} %get-tuple-element.11.refs_4_), channel_id=1, source_target_pairs={{0,1},{1,2},{2,3},{3,0},{4,5},{5,6},{6,7},{7,4},{8,9},{9,10},{10,1... | collective-permute-start | bytes 786440 | tf_op jit(solution)/shard_map/ppermute | solution.py:300
  4.5 2.6 %collective-permute-start.15 = (bf16[128,1024]{1,0:T(8,128)(2,1)S(1)}, bf16[128,1024]{1,0:T(8,128)(2,1)S(1)}, u32[]{:S(2)}, u32[]{:S(2)}) collective-permute-start(bf16[128,1024]{1,0:T(8,128)(2,1)S(1)} %get-tuple-element.12.refs_4_), channel_id=1, source_target_pairs={{0,2},{1,3},{2,0},{3,1},{4,6},{5,7},{6,4},{7,5},{8,10},{9,11},{10,... | collective-permute-start | bytes 786440 | tf_op jit(solution)/shard_map/ppermute | solution.py:300
  10.9 13.5 %collective-permute-done = f32[1,1152]{1,0:T(1,128)S(1)} collective-permute-done((f32[1,1152]{1,0:T(1,128)S(1)}, f32[1,1152]{1,0:T(1,128)S(1)}, u32[]{:S(2)}, u32[]{:S(2)}) %collective-permute-start) | collective-permute-done | bytes 4640 | tf_op jit(solution)/shard_map/ppermute | solution.py:300
  24.4 5.5 %collective-permute-done.1 = f32[1,1152]{1,0:T(1,128)S(1)} collective-permute-done((f32[1,1152]{1,0:T(1,128)S(1)}, f32[1,1152]{1,0:T(1,128)S(1)}, u32[]{:S(2)}, u32[]{:S(2)}) %collective-permute-start.1) | collective-permute-done | bytes 4640 | tf_op jit(solution)/shard_map/ppermute | solution.py:300
  31.5 1.6 collective-permute-start.41
  34.4 2.5 %collective-permute-start.6 = (bf16[128,1024]{1,0:T(8,128)(2,1)S(1)}, bf16[128,1024]{1,0:T(8,128)(2,1)S(1)}, u32[]{:S(2)}, u32[]{:S(2)}) collective-permute-start(bf16[128,1024]{1,0:T(8,128)(2,1)S(1)} %get-tuple-element.14.refs_4_.refs_8_), channel_id=1, source_target_pairs={{0,3},{1,0},{2,1},{3,2},{4,7},{5,4},{6,5},{7,6},{8,11},{9,8},{10,9... | collective-permute-start | bytes 786440 | tf_op jit(solution)/shard_map/ppermute | solution.py:300
  42.1 2.0 %collective-permute-done.36.refs_5_ = bf16[128,1024]{1,0:T(8,128)(2,1)S(1)} collective-permute-done((bf16[128,1024]{1,0:T(8,128)(2,1)S(1)}, bf16[128,1024]{1,0:T(8,128)(2,1)S(1)}, u32[]{:S(2)}, u32[]{:S(2)}) %collective-permute-start.36) | collective-permute-done | bytes 262176 | tf_op jit(solution)/shard_map/ppermute | solution.py:300
  44.6 4.3 %collective-permute-done.6.refs_7_ = bf16[128,1024]{1,0:T(8,128)(2,1)S(1)} collective-permute-done((bf16[128,1024]{1,0:T(8,128)(2,1)S(1)}, bf16[128,1024]{1,0:T(8,128)(2,1)S(1)}, u32[]{:S(2)}, u32[]{:S(2)}) %collective-permute-start.6) | collective-permute-done | bytes 262176 | tf_op jit(solution)/shard_map/ppermute | solution.py:300
  49.8 4.7 %collective-permute-done.33.refs_7_ = bf16[128,1024]{1,0:T(8,128)(2,1)S(1)} collective-permute-done((bf16[128,1024]{1,0:T(8,128)(2,1)S(1)}, bf16[128,1024]{1,0:T(8,128)(2,1)S(1)}, u32[]{:S(2)}, u32[]{:S(2)}) %collective-permute-start.33) | collective-permute-done | bytes 262176 | tf_op jit(solution)/shard_map/ppermute | solution.py:300
  54.4 5.7 %collective-permute-done.9.refs_5_ = bf16[128,1024]{1,0:T(8,128)(2,1)S(1)} collective-permute-done((bf16[128,1024]{1,0:T(8,128)(2,1)S(1)}, bf16[128,1024]{1,0:T(8,128)(2,1)S(1)}, u32[]{:S(2)}, u32[]{:S(2)}) %collective-permute-start.9) | collective-permute-done | bytes 262176 | tf_op jit(solution)/shard_map/ppermute | solution.py:300
  61.3 1.6 collective-permute-start.43
  63.6 6.2 %collective-permute-done.42.refs_5_ = bf16[128,1024]{1,0:T(8,128)(2,1)S(1)} collective-permute-done((bf16[128,1024]{1,0:T(8,128)(2,1)S(1)}, bf16[128,1024]{1,0:T(8,128)(2,1)S(1)}, u32[]{:S(2)}, u32[]{:S(2)}) %collective-permute-start.42) | collective-permute-done | bytes 262176 | tf_op jit(solution)/shard_map/ppermute | solution.py:300
  70.5 5.0 %collective-permute-done.43.refs_6_ = bf16[128,1024]{1,0:T(8,128)(2,1)S(1)} collective-permute-done((bf16[128,1024]{1,0:T(8,128)(2,1)S(1)}, bf16[128,1024]{1,0:T(8,128)(2,1)S(1)}, u32[]{:S(2)}, u32[]{:S(2)}) %collective-permute-start.43) | collective-permute-done | bytes 262176 | tf_op jit(solution)/shard_map/ppermute | solution.py:300
  78.0 2.5 %collective-permute-start.38 = (bf16[128,1024]{1,0:T(8,128)(2,1)S(1)}, bf16[128,1024]{1,0:T(8,128)(2,1)S(1)}, u32[]{:S(2)}, u32[]{:S(2)}) collective-permute-start(bf16[128,1024]{1,0:T(8,128)(2,1)S(1)} %collective-permute-done.16.refs_7_.refs_11_), channel_id=1, source_target_pairs={{0,3},{1,0},{2,1},{3,2},{4,7},{5,4},{6,5},{7,6},{8,11},{9,8},{10,9... | collective-permute-start | bytes 786440 | tf_op jit(solution)/shard_map/ppermute | solution.py:300
  82.2 6.8 %chunk.8 = (f32[4,4,128,1024]{3,2,1,0:T(8,128)}, bf16[512,1024]{1,0:T(8,128)(2,1)S(1)}, bf16[512,3072]{1,0:T(8,128)(2,1)S(1)}) custom-call(s32[3]{0:T(128)S(1)} %add_add_fusion.1.refs_0_, f32[4,4]{1,0:T(4,128)S(1)} %copy-done, f32[4,1024]{1,0:T(4,128)S(1)} %multiply_exponential_fusion.1.refs_2_, f32[4,3072]{1,0:T(4,128)S(1)} %multiply_exponential_fusion.refs_3_, ...), custom_call_target="tpu_custom_call" | custom-call | flops 2147483648 | bytes 6291456 | tf_op jit(solution)/shard_map/chunk/pallas_call | solution.py:243
  89.2 5.7 %chunk.9.refs_10_ = f32[4,4,128,1024]{3,2,1,0:T(8,128)} custom-call(s32[3]{0:T(128)S(1)} %add_add_fusion.7.refs_0_, f32[4,4]{1,0:T(4,128)S(1)} %copy-done, f32[4,1024]{1,0:T(4,128)S(1)} %multiply_exponential_fusion.1.refs_2_, f32[4,3072]{1,0:T(4,128)S(1)} %multiply_exponential_fusion.refs_3_, ...), custom_call_target="tpu_custom_call", output_to_operand_aliasing={{}: (10, {})} | custom-call | flops 2147483648 | bytes 6291456 | tf_op jit(solution)/shard_map/chunk/pallas_call | solution.py:243
  95.0 1.6 collective-permute-start.29
  97.1 1.5 collective-permute-start.37
  99.1 5.7 %chunk.10.refs_10_ = f32[4,4,128,1024]{3,2,1,0:T(8,128)} custom-call(s32[3]{0:T(128)S(1)} %add_add_fusion.6.refs_0_, f32[4,4]{1,0:T(4,128)S(1)} %copy-done, f32[4,1024]{1,0:T(4,128)S(1)} %multiply_exponential_fusion.1.refs_2_, f32[4,3072]{1,0:T(4,128)S(1)} %multiply_exponential_fusion.refs_3_, ...), custom_call_target="tpu_custom_call", output_to_operand_aliasing={{}: (10, {})} | custom-call | flops 2147483648 | bytes 6291456 | tf_op jit(solution)/shard_map/chunk/pallas_call | solution.py:243
  104.9 1.6 collective-permute-start.30
  106.4 5.7 %chunk.11.refs_10_ = f32[4,4,128,1024]{3,2,1,0:T(8,128)} custom-call(s32[3]{0:T(128)S(1)} %add_add_fusion.5.refs_0_, f32[4,4]{1,0:T(4,128)S(1)} %copy-done, f32[4,1024]{1,0:T(4,128)S(1)} %multiply_exponential_fusion.1.refs_2_, f32[4,3072]{1,0:T(4,128)S(1)} %multiply_exponential_fusion.refs_3_, ...), custom_call_target="tpu_custom_call", output_to_operand_aliasing={{}: (10, {})} | custom-call | flops 2147483648 | bytes 6291456 | tf_op jit(solution)/shard_map/chunk/pallas_call | solution.py:243
  112.3 3.2 %collective-permute-done.37.refs_5_ = bf16[128,1024]{1,0:T(8,128)(2,1)S(1)} collective-permute-done((bf16[128,1024]{1,0:T(8,128)(2,1)S(1)}, bf16[128,1024]{1,0:T(8,128)(2,1)S(1)}, u32[]{:S(2)}, u32[]{:S(2)}) %collective-permute-start.37) | collective-permute-done | bytes 262176 | tf_op jit(solution)/shard_map/ppermute | solution.py:300
  115.4 3.8 %collective-permute-start.7 = (bf16[64,1024]{1,0:T(8,128)(2,1)S(1)}, bf16[64,1024]{1,0:T(8,128)(2,1)S(1)}, u32[]{:S(2)}, u32[]{:S(2)}) collective-permute-start(bf16[64,1024]{1,0:T(8,128)(2,1)S(1)} %slice.25), channel_id=1, source_target_pairs={{0,3},{1,0},{2,1},{3,2},{4,7},{5,4},{6,5},{7,6},{8,11},{9,8},{10,9... | collective-permute-start | bytes 393224 | tf_op jit(solution)/shard_map/ppermute | solution.py:300
  119.2 1.5 collective-permute-start.34
  121.1 1.5 collective-permute-start.32
  122.6 5.7 %chunk.12.refs_11_ = f32[4,4,128,1024]{3,2,1,0:T(8,128)} custom-call(s32[3]{0:T(128)S(1)} %add_add_fusion.4.refs_0_, f32[4,4]{1,0:T(4,128)S(1)} %copy-done, f32[4,1024]{1,0:T(4,128)S(1)} %multiply_exponential_fusion.1.refs_2_, f32[4,3072]{1,0:T(4,128)S(1)} %multiply_exponential_fusion.refs_3_, ...), custom_call_target="tpu_custom_call", output_to_operand_aliasing={{}: (10, {})} | custom-call | flops 2147483648 | bytes 6291456 | tf_op jit(solution)/shard_map/chunk/pallas_call | solution.py:243
  128.9 1.5 collective-permute-start.13
  130.9 5.8 %chunk.13.refs_10_ = f32[4,4,128,1024]{3,2,1,0:T(8,128)} custom-call(s32[3]{0:T(128)S(1)} %add_add_fusion.3.refs_0_, f32[4,4]{1,0:T(4,128)S(1)} %copy-done, f32[4,1024]{1,0:T(4,128)S(1)} %multiply_exponential_fusion.1.refs_2_, f32[4,3072]{1,0:T(4,128)S(1)} %multiply_exponential_fusion.refs_3_, ...), custom_call_target="tpu_custom_call", output_to_operand_aliasing={{}: (11, {})} | custom-call | flops 2147483648 | bytes 6291456 | tf_op jit(solution)/shard_map/chunk/pallas_call | solution.py:243
  136.7 1.6 collective-permute-start.11
  139.4 5.7 %chunk.14.refs_11_ = f32[4,4,128,1024]{3,2,1,0:T(8,128)} custom-call(s32[3]{0:T(128)S(1)} %get-tuple-element.16.refs_0_, f32[4,4]{1,0:T(4,128)S(1)} %copy-done, f32[4,1024]{1,0:T(4,128)S(1)} %multiply_exponential_fusion.1.refs_2_, f32[4,3072]{1,0:T(4,128)S(1)} %multiply_exponential_fusion.refs_3_, ...), custom_call_target="tpu_custom_call", output_to_operand_aliasing={{}: (10, {})} | custom-call | flops 2147483648 | bytes 6291456 | tf_op jit(solution)/shard_map/chunk/pallas_call | solution.py:243
  145.2 10.0 %collective-permute-done.11.refs_7_ = bf16[64,1024]{1,0:T(8,128)(2,1)S(1)} collective-permute-done((bf16[64,1024]{1,0:T(8,128)(2,1)S(1)}, bf16[64,1024]{1,0:T(8,128)(2,1)S(1)}, u32[]{:S(2)}, u32[]{:S(2)}) %collective-permute-start.11) | collective-permute-done | bytes 131104 | tf_op jit(solution)/shard_map/ppermute | solution.py:300
  156.6 5.8 %chunk.15 = f32[4,4,128,1024]{3,2,1,0:T(8,128)} custom-call(s32[3]{0:T(128)S(1)} %get-tuple-element.15.refs_0_, f32[4,4]{1,0:T(4,128)S(1)} %copy-done, f32[4,1024]{1,0:T(4,128)S(1)} %multiply_exponential_fusion.1.refs_2_, f32[4,3072]{1,0:T(4,128)S(1)} %multiply_exponential_fusion.refs_3_, ...), custom_call_target="tpu_custom_call", output_to_operand_aliasing={{}: (11, {})} | custom-call | flops 2147483648 | bytes 6291456 | tf_op jit(solution)/shard_map/chunk/pallas_call | solution.py:243
  (92 shorter events, 25.9 us)
Async XLA Ops:
  1.3 30.1 %collective-permute-start.14 = (bf16[128,1024]{1,0:T(8,128)(2,1)S(1)}, bf16[128,1024]{1,0:T(8,128)(2,1)S(1)}, u32[]{:S(2)}, u32[]{:S(2)}) collective-permute-start(bf16[128,1024]{1,0:T(8,128)(2,1)S(1)} %get-tuple-element.11.refs_4_), channel_id=1, source_target_pairs={{0,1},{1,2},{2,3},{3,0},{4,5},{5,6},{6,7},{7,4},{8,9},{9,10},{10,1... | collective-permute-start | bytes 786440 | tf_op jit(solution)/shard_map/ppermute | solution.py:300
  4.5 28.6 %collective-permute-start.15 = (bf16[128,1024]{1,0:T(8,128)(2,1)S(1)}, bf16[128,1024]{1,0:T(8,128)(2,1)S(1)}, u32[]{:S(2)}, u32[]{:S(2)}) collective-permute-start(bf16[128,1024]{1,0:T(8,128)(2,1)S(1)} %get-tuple-element.12.refs_4_), channel_id=1, source_target_pairs={{0,2},{1,3},{2,0},{3,1},{4,6},{5,7},{6,4},{7,5},{8,10},{9,11},{10,... | collective-permute-start | bytes 786440 | tf_op jit(solution)/shard_map/ppermute | solution.py:300
  7.0 27.4 %collective-permute-start.16 = (bf16[128,1024]{1,0:T(8,128)(2,1)S(1)}, bf16[128,1024]{1,0:T(8,128)(2,1)S(1)}, u32[]{:S(2)}, u32[]{:S(2)}) collective-permute-start(bf16[128,1024]{1,0:T(8,128)(2,1)S(1)} %get-tuple-element.13.refs_4_), channel_id=1, source_target_pairs={{0,3},{1,0},{2,1},{3,2},{4,7},{5,4},{6,5},{7,6},{8,11},{9,8},{10,9... | collective-permute-start | bytes 786440 | tf_op jit(solution)/shard_map/ppermute | solution.py:300
  9.8 14.6 %collective-permute-start = (f32[1,1152]{1,0:T(1,128)S(1)}, f32[1,1152]{1,0:T(1,128)S(1)}, u32[]{:S(2)}, u32[]{:S(2)}) collective-permute-start(f32[1,1152]{1,0:T(1,128)S(1)} %broadcast_in_dim.9), channel_id=1, source_target_pairs={{0,1},{1,2},{2,3},{3,0},{4,5},{5,6},{6,7},{7,4},{8,9},{9,10},{10,1... | collective-permute-start | bytes 13832 | tf_op jit(solution)/shard_map/ppermute | solution.py:300
  10.5 19.5 %collective-permute-start.1 = (f32[1,1152]{1,0:T(1,128)S(1)}, f32[1,1152]{1,0:T(1,128)S(1)}, u32[]{:S(2)}, u32[]{:S(2)}) collective-permute-start(f32[1,1152]{1,0:T(1,128)S(1)} %broadcast_in_dim.9), channel_id=1, source_target_pairs={{0,2},{1,3},{2,0},{3,1},{4,6},{5,7},{6,4},{7,5},{8,10},{9,11},{10,... | collective-permute-start | bytes 13832 | tf_op jit(solution)/shard_map/ppermute | solution.py:300
  34.4 14.6 %collective-permute-start.6 = (bf16[128,1024]{1,0:T(8,128)(2,1)S(1)}, bf16[128,1024]{1,0:T(8,128)(2,1)S(1)}, u32[]{:S(2)}, u32[]{:S(2)}) collective-permute-start(bf16[128,1024]{1,0:T(8,128)(2,1)S(1)} %get-tuple-element.14.refs_4_.refs_8_), channel_id=1, source_target_pairs={{0,3},{1,0},{2,1},{3,2},{4,7},{5,4},{6,5},{7,6},{8,11},{9,8},{10,9... | collective-permute-start | bytes 786440 | tf_op jit(solution)/shard_map/ppermute | solution.py:300
  37.9 16.5 %collective-permute-start.33 = (bf16[128,1024]{1,0:T(8,128)(2,1)S(1)}, bf16[128,1024]{1,0:T(8,128)(2,1)S(1)}, u32[]{:S(2)}, u32[]{:S(2)}) collective-permute-start(bf16[128,1024]{1,0:T(8,128)(2,1)S(1)} %get-tuple-element.12.refs_4_), channel_id=1, source_target_pairs={{0,3},{1,0},{2,1},{3,2},{4,7},{5,4},{6,5},{7,6},{8,11},{9,8},{10,9... | collective-permute-start | bytes 786440 | tf_op jit(solution)/shard_map/ppermute | solution.py:300
  39.6 20.6 %collective-permute-start.9 = (bf16[128,1024]{1,0:T(8,128)(2,1)S(1)}, bf16[128,1024]{1,0:T(8,128)(2,1)S(1)}, u32[]{:S(2)}, u32[]{:S(2)}) collective-permute-start(bf16[128,1024]{1,0:T(8,128)(2,1)S(1)} %get-tuple-element.14.refs_4_.refs_8_), channel_id=1, source_target_pairs={{0,1},{1,2},{2,3},{3,0},{4,5},{5,6},{6,7},{7,4},{8,9},{9,10},{10,1... | collective-permute-start | bytes 786440 | tf_op jit(solution)/shard_map/ppermute | solution.py:300
  40.6 19.5 %collective-permute-start.22 = (bf16[128,1024]{1,0:T(8,128)(2,1)S(1)}, bf16[128,1024]{1,0:T(8,128)(2,1)}, u32[]{:S(2)}, u32[]{:S(2)}) collective-permute-start(bf16[128,1024]{1,0:T(8,128)(2,1)S(1)} %collective-permute-done.14.refs_5_.refs_9_), channel_id=1, source_target_pairs={{0,8},{4,12},{8,0},{12,4},{1,9},{5,13},{9,1},{13,5},{2,10},{6,14},... | collective-permute-start | bytes 786440 | tf_op jit(solution)/shard_map/ppermute | solution.py:300
  44.1 16.6 %collective-permute-start.23 = (bf16[128,1024]{1,0:T(8,128)(2,1)S(1)}, bf16[128,1024]{1,0:T(8,128)(2,1)}, u32[]{:S(2)}, u32[]{:S(2)}) collective-permute-start(bf16[128,1024]{1,0:T(8,128)(2,1)S(1)} %collective-permute-done.15.refs_6_.refs_10_), channel_id=1, source_target_pairs={{0,8},{4,12},{8,0},{12,4},{1,9},{5,13},{9,1},{13,5},{2,10},{6,14},... | collective-permute-start | bytes 786440 | tf_op jit(solution)/shard_map/ppermute | solution.py:300
  61.3 14.2 %collective-permute-start.43 = (bf16[128,1024]{1,0:T(8,128)(2,1)S(1)}, bf16[128,1024]{1,0:T(8,128)(2,1)S(1)}, u32[]{:S(2)}, u32[]{:S(2)}) collective-permute-start(bf16[128,1024]{1,0:T(8,128)(2,1)S(1)} %collective-permute-done.15.refs_6_.refs_10_), channel_id=1, source_target_pairs={{0,16},{16,0},{1,17},{17,1},{2,18},{18,2},{3,19},{19,3},{4,20},{20... | collective-permute-start | bytes 786440 | tf_op jit(solution)/shard_map/ppermute | solution.py:300
  63.1 13.6 %collective-permute-start.27 = (bf16[128,1024]{1,0:T(8,128)(2,1)}, bf16[128,1024]{1,0:T(8,128)(2,1)S(1)}, u32[]{:S(2)}, u32[]{:S(2)}) collective-permute-start(bf16[128,1024]{1,0:T(8,128)(2,1)} %collective-permute-done.23.refs_18_), channel_id=1, source_target_pairs={{0,4},{4,0},{8,12},{12,8},{1,5},{5,1},{9,13},{13,9},{2,6},{6,2},{1... | collective-permute-start | bytes 786440 | tf_op jit(solution)/shard_map/ppermute | solution.py:300
  63.4 14.6 %collective-permute-start.28 = (bf16[128,1024]{1,0:T(8,128)(2,1)}, bf16[128,1024]{1,0:T(8,128)(2,1)S(1)}, u32[]{:S(2)}, u32[]{:S(2)}) collective-permute-start(bf16[128,1024]{1,0:T(8,128)(2,1)} %collective-permute-done.24.refs_19_), channel_id=1, source_target_pairs={{0,4},{4,0},{8,12},{12,8},{1,5},{5,1},{9,13},{13,9},{2,6},{6,2},{1... | collective-permute-start | bytes 786440 | tf_op jit(solution)/shard_map/ppermute | solution.py:300
  69.8 19.1 %collective-permute-start.44 = (bf16[128,1024]{1,0:T(8,128)(2,1)S(1)}, bf16[128,1024]{1,0:T(8,128)(2,1)S(1)}, u32[]{:S(2)}, u32[]{:S(2)}) collective-permute-start(bf16[128,1024]{1,0:T(8,128)(2,1)S(1)} %collective-permute-done.16.refs_7_.refs_11_), channel_id=1, source_target_pairs={{0,16},{16,0},{1,17},{17,1},{2,18},{18,2},{3,19},{19,3},{4,20},{20... | collective-permute-start | bytes 786440 | tf_op jit(solution)/shard_map/ppermute | solution.py:300
  75.5 19.5 %collective-permute-start.35 = (bf16[128,1024]{1,0:T(8,128)(2,1)S(1)}, bf16[128,1024]{1,0:T(8,128)(2,1)S(1)}, u32[]{:S(2)}, u32[]{:S(2)}) collective-permute-start(bf16[128,1024]{1,0:T(8,128)(2,1)S(1)} %get-tuple-element.11.refs_4_), channel_id=1, source_target_pairs={{0,16},{16,0},{1,17},{17,1},{2,18},{18,2},{3,19},{19,3},{4,20},{20... | collective-permute-start | bytes 786440 | tf_op jit(solution)/shard_map/ppermute | solution.py:300
  76.0 20.6 %collective-permute-start.12 = (bf16[128,1024]{1,0:T(8,128)(2,1)S(1)}, bf16[128,1024]{1,0:T(8,128)(2,1)S(1)}, u32[]{:S(2)}, u32[]{:S(2)}) collective-permute-start(bf16[128,1024]{1,0:T(8,128)(2,1)S(1)} %get-tuple-element.11.refs_4_), channel_id=1, source_target_pairs={{0,3},{1,0},{2,1},{3,2},{4,7},{5,4},{6,5},{7,6},{8,11},{9,8},{10,9... | collective-permute-start | bytes 786440 | tf_op jit(solution)/shard_map/ppermute | solution.py:300
  76.7 20.4 %collective-permute-start.4 = (bf16[128,1024]{1,0:T(8,128)(2,1)S(1)}, bf16[128,1024]{1,0:T(8,128)(2,1)S(1)}, u32[]{:S(2)}, u32[]{:S(2)}) collective-permute-start(bf16[128,1024]{1,0:T(8,128)(2,1)S(1)} %get-tuple-element.13.refs_4_), channel_id=1, source_target_pairs={{0,1},{1,2},{2,3},{3,0},{4,5},{5,6},{6,7},{7,4},{8,9},{9,10},{10,1... | collective-permute-start | bytes 786440 | tf_op jit(solution)/shard_map/ppermute | solution.py:300
  78.0 20.6 %collective-permute-start.38 = (bf16[128,1024]{1,0:T(8,128)(2,1)S(1)}, bf16[128,1024]{1,0:T(8,128)(2,1)S(1)}, u32[]{:S(2)}, u32[]{:S(2)}) collective-permute-start(bf16[128,1024]{1,0:T(8,128)(2,1)S(1)} %collective-permute-done.16.refs_7_.refs_11_), channel_id=1, source_target_pairs={{0,3},{1,0},{2,1},{3,2},{4,7},{5,4},{6,5},{7,6},{8,11},{9,8},{10,9... | collective-permute-start | bytes 786440 | tf_op jit(solution)/shard_map/ppermute | solution.py:300
  89.0 15.9 %collective-permute-start.31 = (bf16[128,1024]{1,0:T(8,128)(2,1)S(1)}, bf16[128,1024]{1,0:T(8,128)(2,1)S(1)}, u32[]{:S(2)}, u32[]{:S(2)}) collective-permute-start(bf16[128,1024]{1,0:T(8,128)(2,1)S(1)} %collective-permute-done.14.refs_5_.refs_9_), channel_id=1, source_target_pairs={{0,1},{1,2},{2,3},{3,0},{4,5},{5,6},{6,7},{7,4},{8,9},{9,10},{10,1... | collective-permute-start | bytes 786440 | tf_op jit(solution)/shard_map/ppermute | solution.py:300
  95.0 17.2 %collective-permute-start.29 = (bf16[128,1024]{1,0:T(8,128)(2,1)S(1)}, bf16[128,1024]{1,0:T(8,128)(2,1)S(1)}, u32[]{:S(2)}, u32[]{:S(2)}) collective-permute-start(bf16[128,1024]{1,0:T(8,128)(2,1)S(1)} %get-tuple-element.13.refs_4_), channel_id=1, source_target_pairs={{0,16},{16,0},{1,17},{17,1},{2,18},{18,2},{3,19},{19,3},{4,20},{20... | collective-permute-start | bytes 786440 | tf_op jit(solution)/shard_map/ppermute | solution.py:300
  96.6 22.7 %collective-permute-start.40 = (bf16[128,1024]{1,0:T(8,128)(2,1)S(1)}, bf16[128,1024]{1,0:T(8,128)(2,1)S(1)}, u32[]{:S(2)}, u32[]{:S(2)}) collective-permute-start(bf16[128,1024]{1,0:T(8,128)(2,1)S(1)} %collective-permute-done.6.refs_7_), channel_id=1, source_target_pairs={{0,16},{16,0},{1,17},{17,1},{2,18},{18,2},{3,19},{19,3},{4,20},{20... | collective-permute-start | bytes 786440 | tf_op jit(solution)/shard_map/ppermute | solution.py:300
  97.1 18.4 %collective-permute-start.37 = (bf16[128,1024]{1,0:T(8,128)(2,1)S(1)}, bf16[128,1024]{1,0:T(8,128)(2,1)S(1)}, u32[]{:S(2)}, u32[]{:S(2)}) collective-permute-start(bf16[128,1024]{1,0:T(8,128)(2,1)S(1)} %collective-permute-done.36.refs_5_), channel_id=1, source_target_pairs={{0,16},{16,0},{1,17},{17,1},{2,18},{18,2},{3,19},{19,3},{4,20},{20... | collective-permute-start | bytes 786440 | tf_op jit(solution)/shard_map/ppermute | solution.py:300
  98.6 22.5 %collective-permute-start.39 = (bf16[128,1024]{1,0:T(8,128)(2,1)S(1)}, bf16[128,1024]{1,0:T(8,128)(2,1)S(1)}, u32[]{:S(2)}, u32[]{:S(2)}) collective-permute-start(bf16[128,1024]{1,0:T(8,128)(2,1)S(1)} %collective-permute-done.38.refs_6_), channel_id=1, source_target_pairs={{0,16},{16,0},{1,17},{17,1},{2,18},{18,2},{3,19},{19,3},{4,20},{20... | collective-permute-start | bytes 786440 | tf_op jit(solution)/shard_map/ppermute | solution.py:300
  104.9 25.6 %collective-permute-start.30 = (bf16[128,1024]{1,0:T(8,128)(2,1)S(1)}, bf16[128,1024]{1,0:T(8,128)(2,1)S(1)}, u32[]{:S(2)}, u32[]{:S(2)}) collective-permute-start(bf16[128,1024]{1,0:T(8,128)(2,1)S(1)} %collective-permute-done.9.refs_5_), channel_id=1, source_target_pairs={{0,16},{16,0},{1,17},{17,1},{2,18},{18,2},{3,19},{19,3},{4,20},{20... | collective-permute-start | bytes 786440 | tf_op jit(solution)/shard_map/ppermute | solution.py:300
  112.2 16.1 %collective-permute-start.10 = (bf16[64,1024]{1,0:T(8,128)(2,1)S(1)}, bf16[64,1024]{1,0:T(8,128)(2,1)S(1)}, u32[]{:S(2)}, u32[]{:S(2)}) collective-permute-start(bf16[64,1024]{1,0:T(8,128)(2,1)S(1)} %slice.26), channel_id=1, source_target_pairs={{0,1},{1,2},{2,3},{3,0},{4,5},{5,6},{6,7},{7,4},{8,9},{9,10},{10,1... | collective-permute-start | bytes 393224 | tf_op jit(solution)/shard_map/ppermute | solution.py:300
  119.2 17.5 %collective-permute-start.34 = (bf16[128,1024]{1,0:T(8,128)(2,1)S(1)}, bf16[128,1024]{1,0:T(8,128)(2,1)S(1)}, u32[]{:S(2)}, u32[]{:S(2)}) collective-permute-start(bf16[128,1024]{1,0:T(8,128)(2,1)S(1)} %collective-permute-done.33.refs_7_), channel_id=1, source_target_pairs={{0,16},{16,0},{1,17},{17,1},{2,18},{18,2},{3,19},{19,3},{4,20},{20... | collective-permute-start | bytes 786440 | tf_op jit(solution)/shard_map/ppermute | solution.py:300
  121.1 17.3 %collective-permute-start.32 = (bf16[128,1024]{1,0:T(8,128)(2,1)S(1)}, bf16[128,1024]{1,0:T(8,128)(2,1)S(1)}, u32[]{:S(2)}, u32[]{:S(2)}) collective-permute-start(bf16[128,1024]{1,0:T(8,128)(2,1)S(1)} %collective-permute-done.31.refs_6_), channel_id=1, source_target_pairs={{0,16},{16,0},{1,17},{17,1},{2,18},{18,2},{3,19},{19,3},{4,20},{20... | collective-permute-start | bytes 786440 | tf_op jit(solution)/shard_map/ppermute | solution.py:300
  128.3 16.8 %collective-permute-start.3 = (bf16[128,1024]{1,0:T(8,128)(2,1)S(1)}, bf16[128,1024]{1,0:T(8,128)(2,1)S(1)}, u32[]{:S(2)}, u32[]{:S(2)}) collective-permute-start(bf16[128,1024]{1,0:T(8,128)(2,1)S(1)} %get-tuple-element.12.refs_4_), channel_id=1, source_target_pairs={{0,16},{16,0},{1,17},{17,1},{2,18},{18,2},{3,19},{19,3},{4,20},{20... | collective-permute-start | bytes 786440 | tf_op jit(solution)/shard_map/ppermute | solution.py:300
  128.9 27.7 %collective-permute-start.13 = (bf16[128,1024]{1,0:T(8,128)(2,1)S(1)}, bf16[128,1024]{1,0:T(8,128)(2,1)S(1)}, u32[]{:S(2)}, u32[]{:S(2)}) collective-permute-start(bf16[128,1024]{1,0:T(8,128)(2,1)S(1)} %collective-permute-done.12.refs_8_), channel_id=1, source_target_pairs={{0,16},{16,0},{1,17},{17,1},{2,18},{18,2},{3,19},{19,3},{4,20},{20... | collective-permute-start | bytes 786440 | tf_op jit(solution)/shard_map/ppermute | solution.py:300
  130.4 26.2 %collective-permute-start.5 = (bf16[128,1024]{1,0:T(8,128)(2,1)S(1)}, bf16[128,1024]{1,0:T(8,128)(2,1)S(1)}, u32[]{:S(2)}, u32[]{:S(2)}) collective-permute-start(bf16[128,1024]{1,0:T(8,128)(2,1)S(1)} %collective-permute-done.4.refs_5_), channel_id=1, source_target_pairs={{0,16},{16,0},{1,17},{17,1},{2,18},{18,2},{3,19},{19,3},{4,20},{20... | collective-permute-start | bytes 786440 | tf_op jit(solution)/shard_map/ppermute | solution.py:300
  136.7 18.5 %collective-permute-start.11 = (bf16[64,1024]{1,0:T(8,128)(2,1)S(1)}, bf16[64,1024]{1,0:T(8,128)(2,1)S(1)}, u32[]{:S(2)}, u32[]{:S(2)}) collective-permute-start(bf16[64,1024]{1,0:T(8,128)(2,1)S(1)} %collective-permute-done.10.refs_7_), channel_id=1, source_target_pairs={{0,16},{16,0},{1,17},{17,1},{2,18},{18,2},{3,19},{19,3},{4,20},{20... | collective-permute-start | bytes 393224 | tf_op jit(solution)/shard_map/ppermute | solution.py:300
  138.3 18.3 %collective-permute-start.8 = (bf16[64,1024]{1,0:T(8,128)(2,1)S(1)}, bf16[64,1024]{1,0:T(8,128)(2,1)S(1)}, u32[]{:S(2)}, u32[]{:S(2)}) collective-permute-start(bf16[64,1024]{1,0:T(8,128)(2,1)S(1)} %collective-permute-done.7.refs_6_), channel_id=1, source_target_pairs={{0,16},{16,0},{1,17},{17,1},{2,18},{18,2},{3,19},{19,3},{4,20},{20... | collective-permute-start | bytes 393224 | tf_op jit(solution)/shard_map/ppermute | solution.py:300
  (16 other events, 107.6 us)

commit v2 on v0

v2 whole, which is shorter than its diff:
```python
import functools

import jax
import jax.numpy as jnp
from jax import lax
from jax.experimental import pallas as pl
from jax.experimental.pallas import tpu as pltpu
from jax.sharding import PartitionSpec as P


LANES = 128


def make_plan(n, rows, cols):
    plan, known = [], set()
    near = sorted(range(1, n), key=lambda k: (min(k, n - k), k))
    late = [m for pair in zip(range(1, n), range(n - 1, 0, -1)) for m in pair]
    late = list(dict.fromkeys(late))
    ends = near[:2]
    groups = [[0, *ends]] + [[k] for k in near[2:]]

    def emit(axis, shift, source, target):
        if target not in known:
            known.add(target)
            plan.append(("move", axis, shift, source, target))

    def direct(m, k):
        return m == 0 or k in ends

    def own(m, k, dy=None):
        at = (lambda *key: ("Y", dy, *key)) if dy else (lambda *key: ("P", *key))
        start = (lambda d: ("Y", dy, d, 0)) if dy else (lambda d: ("S", d))
        if direct(m, k):
            shift = k if 2 * k <= n else k - n
            emit("tm", shift, start((k + m) % n), at(m, k))
        elif 2 * k < n or (2 * k == n and 2 * m > n):
            own((m + 1) % n, k - 1, dy)
            emit("tm", 1, at((m + 1) % n, k - 1), at(m, k))
        else:
            own(m - 1, k + 1, dy)
            emit("tm", -1, at(m - 1, k + 1), at(m, k))

    def across(m, ks):
        for dy in range(1, rows):
            for k in ks:
                emit("row", dy, ("P", m, k) if k else ("S", m), ("Y", dy, m, k))

    def spread(g, ds):
        for d in ds:
            if d & 1 and d > 1:
                emit("col", 1, ("F", d - 1, g), ("F", d, g))
            else:
                emit("col", d, ("F", 0, g), ("F", d, g))

    def kernel(*chunks):
        plan.append(("kernel", chunks))

    even, odd = range(2, cols, 2), range(3, cols, 2)
    others = range(1, rows)
    for k in near:
        own(0, k)
    for m in late:
        across(m, [0])
    for k in ends:
        own(late[0], k)
    for k in near:
        plan.append(("move", "tm", k, ("D", 0), ("D", k)))
    for g in range(len(groups)):
        spread(g, even)
        for dy in others:
            emit("row", dy, ("F", 0, g), ("Y", dy, "F", g))
        spread(g, [1] if cols > 1 else [])
        if g == 0:
            for m in late[:2]:
                for k in near:
                    own(m, k)
    for g in range(len(groups)):
        spread(g, odd)
    last = late[-1]
    kernel((0, 0))
    across(late[0], near)
    for m in late[2:]:
        for k in reversed(near):
            own(m, k)
    kernel(*[(dy, 0) for dy in others], (0, late[0]))
    for dy in others:
        for k in ends:
            own(last, k, dy)
    for m in late[1:-1]:
        across(m, near)
    kernel((0, late[1]), *[(dy, late[0]) for dy in others])
    across(last, [k for k in near if k not in ends])
    for m in late[1:-1]:
        kernel(*[(dy, m) for dy in others])
    for m in late[2:]:
        kernel((0, m))
    kernel(*[(dy, last) for dy in others])
    return plan, groups


def chunk_kernel(chunks, blocks, count, *refs):
    refs = list(refs)
    place, cosines, scale_o, scale_e = refs[:4]
    used = 1 + max(piece[0] for piece in [*blocks, *(p for c in chunks for p in c)])
    sources, rest = refs[4 : 4 + used], refs[4 + used :]
    freqs, times = cosines.shape
    if blocks:
        out, keep_o, keep_e = rest[:3]
        rest = rest[3:]
    else:
        kept_o, kept_e, _, out = rest[:4]
        rest = rest[4:]
    fo, fe, co, ce, so, se, go, ge, ob, piece_sem, first_sem, out_sem, keep_sem = rest
    bo, be = co.shape[2] // count, ce.shape[2] // count
    width = co.shape[1]
    cols = fo.shape[0] // width

    def pair(piece, into_o, into_e, sem, i):
        source, there, start, size, at = piece
        rows, there = pl.ds(start, size), pl.ds(there, size)
        source = sources[source]
        return [
            pltpu.make_async_copy(
                source.at[there, pl.ds(0, bo)],
                into_o.at[rows, pl.ds(at * bo, bo)],
                sem.at[2 * i],
            ),
            pltpu.make_async_copy(
                source.at[there, pl.ds(bo, be)],
                into_e.at[rows, pl.ds(at * be, be)],
                sem.at[2 * i + 1],
            ),
        ]

    loads = [
        [
            copy
            for i, piece in enumerate(pieces)
            for copy in pair(piece, co.at[j], ce.at[j], piece_sem.at[j], i)
        ]
        for j, pieces in enumerate(chunks)
    ]
    if blocks:
        firsts = [
            copy
            for i, piece in enumerate(blocks)
            for copy in pair(piece, fo, fe, first_sem, i)
        ]
    else:
        firsts = [
            pltpu.make_async_copy(kept_o, fo, first_sem.at[0]),
            pltpu.make_async_copy(kept_e, fe, first_sem.at[1]),
        ]
    for copy in [*loads[0], *firsts, *(c for later in loads[1:] for c in later)]:
        copy.start()

    step, tall = 16, 64
    contract = (((1,), (1,)), ((), ()))
    column, z = place[0], place[1]
    weights = [
        [-cosines[f, lax.rem(z + times - t, times)] for t in range(times)] for f in range(freqs)
    ]
    keeps, puts = [], []
    for j in range(len(chunks)):
        for copy in loads[j]:
            copy.wait()

        @pl.loop(0, width // step)
        def _(i, j=j):
            rows = pl.ds(pl.multiple_of(i * step, step), step)
            for source, scale, into in ((co, scale_o, so), (ce, scale_e, se)):
                wide = source[j, rows, :].astype(jnp.float32)
                for t in range(times):
                    at = pl.ds(pl.multiple_of(t * width + i * step, step), step)
                    into[at, :] = (wide * scale[t : t + 1, :]).astype(jnp.bfloat16)

        if j == 0:
            for copy in firsts:
                copy.wait()
            if blocks:
                keeps = [
                    pltpu.make_async_copy(fo, keep_o, keep_sem.at[0]),
                    pltpu.make_async_copy(fe, keep_e, keep_sem.at[1]),
                ]
                for copy in keeps:
                    copy.start()
        go[...] = lax.dot_general(fo[...], so[...], contract, preferred_element_type=jnp.float32)
        ge[...] = lax.dot_general(fe[...], se[...], contract, preferred_element_type=jnp.float32)
        lane = pl.ds(pl.multiple_of(place[2 + j] * width, width), width)
        for d in range(cols):
            q = jnp.bitwise_xor(column, d)

            @pl.loop(0, width // tall)
            def _(i, d=d, q=q, j=j):
                rows = pl.ds(pl.multiple_of(d * width + i * tall, tall), tall)
                into = pl.ds(pl.multiple_of(i * tall, tall), tall)
                totals = [None] * freqs
                for t in range(times):
                    lanes = pl.ds(t * width, width)
                    polar = (go[rows, lanes] * ge[rows, lanes]).astype(jnp.bfloat16)
                    polar = polar.astype(jnp.float32)
                    for f in range(freqs):
                        term = weights[f][t] * polar
                        totals[f] = term if t == 0 else totals[f] + term
                for f in range(freqs):
                    ob[j, f, d, into, :] = totals[f]

            put = pltpu.make_async_copy(
                ob.at[j, :, d], out.at[:, q, :, lane], out_sem.at[j * cols + d]
            )
            put.start()
            puts.append(put)
    for copy in [*keeps, *puts]:
        copy.wait()


def chunk_call(place, cosines, scales, sources, chunks, blocks, kept, out, shape, count):
    freqs, cols, width, _ = shape
    times = cosines.shape[1]
    ko, ke = scales[0].shape[1], scales[1].shape[1]
    tile = cols * width
    many = len(chunks)
    hbm = pl.BlockSpec(memory_space=pl.ANY)
    smem = pl.BlockSpec(memory_space=pltpu.SMEM)
    vmem = pl.BlockSpec(memory_space=pltpu.VMEM)
    result = jax.ShapeDtypeStruct(shape, jnp.float32)
    operands = [place, cosines, *scales, *sources]
    in_specs = [smem, smem, vmem, vmem] + [hbm] * len(sources)
    if blocks:
        out_shape = (
            result,
            jax.ShapeDtypeStruct((tile, ko), jnp.bfloat16),
            jax.ShapeDtypeStruct((tile, ke), jnp.bfloat16),
        )
        out_specs = (hbm, hbm, hbm)
        aliases = {}
    else:
        operands += [*kept, out]
        in_specs += [hbm] * 3
        out_shape, out_specs = result, hbm
        aliases = {len(operands) - 1: 0}
    return pl.pallas_call(
        functools.partial(chunk_kernel, chunks, blocks, count),
        out_shape=out_shape,
        in_specs=in_specs,
        out_specs=out_specs,
        input_output_aliases=aliases,
        scratch_shapes=[
            pltpu.VMEM((tile, ko), jnp.bfloat16),
            pltpu.VMEM((tile, ke), jnp.bfloat16),
            pltpu.VMEM((many, width, ko), jnp.bfloat16),
            pltpu.VMEM((many, width, ke), jnp.bfloat16),
            pltpu.VMEM((times * width, ko), jnp.bfloat16),
            pltpu.VMEM((times * width, ke), jnp.bfloat16),
            pltpu.VMEM((tile, times * width), jnp.float32),
            pltpu.VMEM((tile, times * width), jnp.float32),
            pltpu.VMEM((many, freqs, cols, width, width), jnp.float32),
            pltpu.SemaphoreType.DMA((many, 2 * count)),
            pltpu.SemaphoreType.DMA((2 * max(1, len(blocks)),)),
            pltpu.SemaphoreType.DMA((many * cols,)),
            pltpu.SemaphoreType.DMA((2,)),
        ],
        compiler_params=pltpu.CompilerParams(vmem_limit_bytes=36 * 2**20),
        cost_estimate=pl.CostEstimate(
            flops=2 * many * tile * times * width * (ko + ke),
            bytes_accessed=2 * (tile + many * width) * (ko + ke) + 4 * many * freqs * tile * width,
            transcendentals=0,
        ),
        name="chunk",
    )(*operands)


def streamed(plan, groups, sizes, filled, empty, filled_depth, empty_depth, time_points, cosines):
    n, rows, cols = sizes["tm"], sizes["row"], sizes["col"]
    z, r, c = lax.axis_index("tm"), lax.axis_index("row"), lax.axis_index("col")
    points, bo = filled.shape[1:]
    be = empty.shape[2]
    width = points // n
    shape = (cosines.shape[0], cols, width, rows * points)
    whole = jnp.concatenate([filled[0], empty[0]], axis=1)
    values = {}
    for d in range(n):
        values["S", d] = lax.dynamic_slice_in_dim(whole, lax.rem(z + d, n) * width, width, 0)
    depth = jnp.concatenate([filled_depth, empty_depth]).astype(jnp.float32)
    values["D", 0] = jnp.concatenate([depth, jnp.broadcast_to(time_points, (LANES,))])[None, :]
    perms = {
        "tm": lambda s: [(i, (i + s) % n) for i in range(n)],
        "row": lambda s: [(i, (i + s) % rows) for i in range(rows)],
        "col": lambda s: [(i, i ^ s) for i in range(cols)],
    }
    home = {k: (g, i) for g, group in enumerate(groups) for i, k in enumerate(group)}

    def lookup(key):
        if key not in values and key[0] == "F" and key[1] == 0:
            parts = [values["P", 0, k] if k else values["S", 0] for k in groups[key[2]]]
            values[key] = parts[0] if len(parts) == 1 else jnp.concatenate(parts, axis=0)
        return values[key]

    def find(dy, m, k):
        if dy and m == 0:
            return lookup(("Y", dy, "F", home[k][0])), home[k][1] * width
        if dy:
            return lookup(("Y", dy, m, k)), 0
        return lookup(("P", m, k) if k else ("S", m)), 0

    scales = kept = out = None
    for step in plan:
        if step[0] == "move":
            _, axis, shift, source, target = step
            values[target] = lax.ppermute(lookup(source), axis, perms[axis](shift))
            continue
        sources = []

        def entry(array, there, row, k):
            for at, other in enumerate(sources):
                if other is array:
                    return (at, there, row, width, k)
            sources.append(array)
            return (len(sources) - 1, there, row, width, k)

        blocks = []
        if scales is None:
            held = [values["D", k] for k in range(n)]
            end = ("F", cols - 1, len(groups) - 1)
            *held, values[end] = lax.optimization_barrier((*held, lookup(end)))
            stacked = jnp.concatenate(held, axis=0)
            deep, tau = stacked[:, : bo + be], stacked[:, bo + be :][:, :1]
            scales = [
                jnp.exp(-piece.reshape(1, -1) * tau) for piece in (deep[:, :bo], deep[:, bo:])
            ]
            for d in range(cols):
                for k in range(n):
                    g, at = home[k]
                    if d:
                        blocks.append(
                            entry(lookup(("F", d, g)), at * width, d * width, k)
                        )
                    else:
                        blocks.append(entry(*find(0, 0, k), 0, k))
        chunks, spots = [], []
        for dy, m in step[1]:
            chunks.append(tuple(entry(*find(dy, m, k), 0, k) for k in range(n)))
            spots.append(lax.rem(r + rows - dy, rows) * n + lax.rem(z + m, n))
        place = jnp.stack([c, z, *spots]).astype(jnp.int32)
        result = chunk_call(
            place, cosines, scales, sources, tuple(chunks), tuple(blocks), kept, out, shape, n
        )
        if blocks:
            out, *kept = result
        else:
            out = result
    return out


def gathered(sizes, filled, empty, filled_depth, empty_depth, time_points, cosines):
    points = filled.shape[1]
    width = points // sizes["tm"]
    z = lax.axis_index("tm")

    def green(orbitals, depths):
        mine = lax.all_gather(orbitals[0], "tm", axis=1, tiled=True)
        depths = lax.all_gather(depths, "tm", axis=0, tiled=True).astype(jnp.float32)
        first = lax.all_gather(
            lax.dynamic_slice_in_dim(mine, z * width, width, 0), "col", axis=0, tiled=True
        )
        second = lax.all_gather(mine, "row", axis=0, tiled=True)

        def at(tau):
            scaled = (second.astype(jnp.float32) * jnp.exp(-depths * tau)[None, :]).astype(
                jnp.bfloat16
            )
            return lax.dot_general(
                first, scaled, (((1,), (1,)), ((), ())), preferred_element_type=jnp.float32
            )

        return at

    taus = lax.all_gather(time_points, "tm", axis=0, tiled=True)
    at_o, at_e = green(filled, filled_depth), green(empty, empty_depth)
    total = 0.0
    for t in range(taus.shape[0]):
        polar = (-(at_o(taus[t]) * at_e(taus[t]))).astype(jnp.bfloat16).astype(jnp.float32)
        total = total + cosines[:, t, None, None] * polar[None]
    return total.reshape(cosines.shape[0], sizes["col"], width, -1)


def solution(mesh):
    sizes = dict(mesh.shape)
    in_specs = (P("col", "row", "tm"), P("col", "row", "tm"), P("tm"), P("tm"), P("tm"), P())
    out_specs = P(None, None, ("row", "tm"), "col")
    plan, groups = make_plan(sizes["tm"], sizes["row"], sizes["col"])

    def on_device(filled, *rest):
        width = filled.shape[1] // sizes["tm"]
        if width % LANES or sizes["col"] & (sizes["col"] - 1):
            return gathered(sizes, filled, *rest)
        return streamed(plan, groups, sizes, filled, *rest)

    return jax.shard_map(
        on_device, mesh=mesh, in_specs=in_specs, out_specs=out_specs, check_vma=False
    )
```

time: 492 us -> 138 us (0.28)
  waiting for transfers between devices: 290 us -> 42.2 us
  blocking collectives: 121 us -> 0 us
  starting transfers between devices: 0.19 us -> 49.1 us
  Pallas kernels: 0 us -> 41.3 us
  matrix products: 40.1 us -> 0 us
  local copies, waits for them, and re-layouts: 26.1 us -> 0.7 us
  between operations: 14.2 us -> 1.04 us
    all_gather x6 -> x0, waiting for transfers between devices: 287 us -> none  [the longest x1 83.5 us: on_device(): lax.all_gather(empty_bands, 'col', axis=0, tiled=True)]
    all_to_all x1 -> x0, blocking collectives: 98.1 us -> none  [on_device(): lax.all_to_all(polar_time[None], 'tm', split_axis=2, concat_axis=0, tiled...]
    ppermute x0 -> x35, starting transfers between devices: none -> 49.1 us  [streamed(): values[target] = lax.ppermute(lookup(source), axis, perms[axis](shift))]
    ppermute x0 -> x35, waiting for transfers between devices: none -> 42.2 us  [streamed(): values[target] = lax.ppermute(lookup(source), axis, perms[axis](shift))]
    pallas_call x0 -> x6, Pallas kernels: none -> 41.3 us  [chunk_call(): pl.pallas_call(functools.partial(chunk_kernel, chunks, blocks, count), ou...]
    dot_general x3 -> x0, matrix products: 40.1 us -> none  [the longest x2 30.6 us: tile_product(): lax.dot_general(left_points.reshape(-1, band_count), scaled, (((1,), (1,)...]
    all_gather x2 -> x0, blocking collectives: 23.2 us -> none  [the longest x1 13.1 us: on_device(): lax.all_gather(empty_depth, 'tm', axis=0, tiled=True)]
    another operation x2 -> x0, local copies, waits for them, and re-layouts: 17.8 us -> none  [on_device(): polar_time[None]]
  transfers between devices with their start and end apart: 6 -> 35, of which waited for: 6 -> 9; matrix products, arithmetic and copies ran while one was open for 4% -> 2% of each run, Pallas kernels for 0% -> 26%
where the time goes in v2:
time: 138 us
  starting transfers between devices  49.1 us (36%)
  waiting for transfers between devices  42.2 us (31%)
  Pallas kernels  41.3 us (30%)
  other arithmetic  3.6 us (3%)
    ppermute x35, starting transfers between devices, streamed(): values[target] = lax.ppermute(lookup(source), axis, perms[axis](shift))  49.1 us
    ppermute x35, waiting for transfers between devices, streamed(): values[target] = lax.ppermute(lookup(source), axis, perms[axis](shift))  42.2 us
    pallas_call x6, Pallas kernels, chunk_call(): pl.pallas_call(functools.partial(chunk_kernel, chunks, blocks, count), ou...  41.3 us
  transfers between devices with their start and end apart: 35, of which 9 were waited for; matrix products, arithmetic and copies ran while one was open for 2% of the time, Pallas kernels for 26%

profile of v2, /device:TPU:0, one launch (start us, length us, event | category | flops | bytes accessed | tf_op | source)
XLA Modules:
  0.0 138.0 jit_solution(11348560722147600386)
XLA Ops:
  1.3 4.1 %collective-permute-start.3 = (bf16[128,1024]{1,0:T(8,128)(2,1)S(1)}, bf16[128,1024]{1,0:T(8,128)(2,1)S(1)}, u32[]{:S(2)}, u32[]{:S(2)}) collective-permute-start(bf16[128,1024]{1,0:T(8,128)(2,1)S(1)} %get-tuple-element.24.refs_4_), channel_id=1, source_target_pairs={{0,2},{1,3},{2,0},{3,1},{4,6},{5,7},{6,4},{7,5},{8,10},{9,11},{10,... | collective-permute-start | bytes 786440 | tf_op jit(solution)/shard_map/ppermute | solution.py:310
  5.5 1.6 %collective-permute-start.14 = (bf16[128,1024]{1,0:T(8,128)(2,1)S(1)}, bf16[128,1024]{1,0:T(8,128)(2,1)S(1)}, u32[]{:S(2)}, u32[]{:S(2)}) collective-permute-start(bf16[128,1024]{1,0:T(8,128)(2,1)S(1)} %get-tuple-element.23.refs_6_), channel_id=1, source_target_pairs={{0,1},{1,2},{2,3},{3,0},{4,5},{5,6},{6,7},{7,4},{8,9},{9,10},{10,1... | collective-permute-start | bytes 786440 | tf_op jit(solution)/shard_map/ppermute | solution.py:310
  7.1 2.2 %collective-permute-start.15 = (bf16[128,1024]{1,0:T(8,128)(2,1)S(1)}, bf16[128,1024]{1,0:T(8,128)(2,1)S(1)}, u32[]{:S(2)}, u32[]{:S(2)}) collective-permute-start(bf16[128,1024]{1,0:T(8,128)(2,1)S(1)} %get-tuple-element.25.refs_4_), channel_id=1, source_target_pairs={{0,3},{1,0},{2,1},{3,2},{4,7},{5,4},{6,5},{7,6},{8,11},{9,8},{10,9... | collective-permute-start | bytes 786440 | tf_op jit(solution)/shard_map/ppermute | solution.py:310
  10.0 14.0 %collective-permute-done.3.refs_6_ = bf16[128,1024]{1,0:T(8,128)(2,1)S(1)} collective-permute-done((bf16[128,1024]{1,0:T(8,128)(2,1)S(1)}, bf16[128,1024]{1,0:T(8,128)(2,1)S(1)}, u32[]{:S(2)}, u32[]{:S(2)}) %collective-permute-start.3) | collective-permute-done | bytes 262176 | tf_op jit(solution)/shard_map/ppermute | solution.py:310
  23.9 1.8 %collective-permute-start.4 = (bf16[128,1024]{1,0:T(8,128)(2,1)S(1)}, bf16[128,1024]{1,0:T(8,128)(2,1)}, u32[]{:S(2)}, u32[]{:S(2)}) collective-permute-start(bf16[128,1024]{1,0:T(8,128)(2,1)S(1)} %collective-permute-done.3.refs_6_), channel_id=1, source_target_pairs={{0,8},{4,12},{8,0},{12,4},{1,9},{5,13},{9,1},{13,5},{2,10},{6,14},... | collective-permute-start | bytes 786440 | tf_op jit(solution)/shard_map/ppermute | solution.py:310
  27.8 4.8 %collective-permute-start = (f32[1,1152]{1,0:T(1,128)S(1)}, f32[1,1152]{1,0:T(1,128)S(1)}, u32[]{:S(2)}, u32[]{:S(2)}) collective-permute-start(f32[1,1152]{1,0:T(1,128)S(1)} %broadcast_in_dim.9), channel_id=1, source_target_pairs={{0,1},{1,2},{2,3},{3,0},{4,5},{5,6},{6,7},{7,4},{8,9},{9,10},{10,1... | collective-permute-start | bytes 13832 | tf_op jit(solution)/shard_map/ppermute | solution.py:310
  32.5 2.0 %collective-permute-start.1 = (f32[1,1152]{1,0:T(1,128)S(1)}, f32[1,1152]{1,0:T(1,128)S(1)}, u32[]{:S(2)}, u32[]{:S(2)}) collective-permute-start(f32[1,1152]{1,0:T(1,128)S(1)} %broadcast_in_dim.9), channel_id=1, source_target_pairs={{0,2},{1,3},{2,0},{3,1},{4,6},{5,7},{6,4},{7,5},{8,10},{9,11},{10,... | collective-permute-start | bytes 13832 | tf_op jit(solution)/shard_map/ppermute | solution.py:310
  34.5 2.8 %collective-permute-start.2 = (f32[1,1152]{1,0:T(1,128)S(1)}, f32[1,1152]{1,0:T(1,128)S(1)}, u32[]{:S(2)}, u32[]{:S(2)}) collective-permute-start(f32[1,1152]{1,0:T(1,128)S(1)} %broadcast_in_dim.9), channel_id=1, source_target_pairs={{0,3},{1,0},{2,1},{3,2},{4,7},{5,4},{6,5},{7,6},{8,11},{9,8},{10,9... | collective-permute-start | bytes 13832 | tf_op jit(solution)/shard_map/ppermute | solution.py:310
  37.6 3.8 %collective-permute-start.9 = (bf16[128,1024]{1,0:T(8,128)(2,1)S(1)}, bf16[128,1024]{1,0:T(8,128)(2,1)S(1)}, u32[]{:S(2)}, u32[]{:S(2)}) collective-permute-start(bf16[128,1024]{1,0:T(8,128)(2,1)S(1)} %get-tuple-element.26.refs_4_), channel_id=1, source_target_pairs={{0,3},{1,0},{2,1},{3,2},{4,7},{5,4},{6,5},{7,6},{8,11},{9,8},{10,9... | collective-permute-start | bytes 786440 | tf_op jit(solution)/shard_map/ppermute | solution.py:310
  41.4 1.5 %collective-permute-start.12 = (bf16[128,1024]{1,0:T(8,128)(2,1)S(1)}, bf16[128,1024]{1,0:T(8,128)(2,1)S(1)}, u32[]{:S(2)}, u32[]{:S(2)}) collective-permute-start(bf16[128,1024]{1,0:T(8,128)(2,1)S(1)} %get-tuple-element.23.refs_6_), channel_id=1, source_target_pairs={{0,16},{16,0},{1,17},{17,1},{2,18},{18,2},{3,19},{19,3},{4,20},{20... | collective-permute-start | bytes 786440 | tf_op jit(solution)/shard_map/ppermute | solution.py:310
  43.3 4.1 %collective-permute-done.18.refs_10_ = bf16[384,1024]{1,0:T(8,128)(2,1)S(1)} collective-permute-done((bf16[384,1024]{1,0:T(8,128)(2,1)}, bf16[384,1024]{1,0:T(8,128)(2,1)S(1)}, u32[]{:S(2)}, u32[]{:S(2)}) %collective-permute-start.18) | collective-permute-done | bytes 786464 | tf_op jit(solution)/shard_map/ppermute | solution.py:310
  50.0 2.0 %collective-permute-done.9.refs_9_ = bf16[128,1024]{1,0:T(8,128)(2,1)S(1)} collective-permute-done((bf16[128,1024]{1,0:T(8,128)(2,1)S(1)}, bf16[128,1024]{1,0:T(8,128)(2,1)S(1)}, u32[]{:S(2)}, u32[]{:S(2)}) %collective-permute-start.9) | collective-permute-done | bytes 262176 | tf_op jit(solution)/shard_map/ppermute | solution.py:310
  52.0 1.5 %collective-permute-start.33 = (bf16[384,1024]{1,0:T(8,128)(2,1)}, bf16[384,1024]{1,0:T(8,128)(2,1)S(1)}, u32[]{:S(2)}, u32[]{:S(2)}) collective-permute-start(bf16[384,1024]{1,0:T(8,128)(2,1)} %pad_maximum_fusion), channel_id=1, source_target_pairs={{0,16},{16,0},{1,17},{17,1},{2,18},{18,2},{3,19},{19,3},{4,20},{20... | collective-permute-start | bytes 2359304 | tf_op jit(solution)/shard_map/ppermute | solution.py:310
  53.6 5.7 %collective-permute-done.22.refs_5_ = bf16[128,1024]{1,0:T(8,128)(2,1)S(1)} collective-permute-done((bf16[128,1024]{1,0:T(8,128)(2,1)S(1)}, bf16[128,1024]{1,0:T(8,128)(2,1)S(1)}, u32[]{:S(2)}, u32[]{:S(2)}) %collective-permute-start.22) | collective-permute-done | bytes 262176 | tf_op jit(solution)/shard_map/ppermute | solution.py:310
  60.3 1.5 %collective-permute-start.7 = (bf16[128,1024]{1,0:T(8,128)(2,1)S(1)}, bf16[128,1024]{1,0:T(8,128)(2,1)S(1)}, u32[]{:S(2)}, u32[]{:S(2)}) collective-permute-start(bf16[128,1024]{1,0:T(8,128)(2,1)S(1)} %get-tuple-element.25.refs_4_), channel_id=1, source_target_pairs={{0,16},{16,0},{1,17},{17,1},{2,18},{18,2},{3,19},{19,3},{4,20},{20... | collective-permute-start | bytes 786440 | tf_op jit(solution)/shard_map/ppermute | solution.py:310
  61.9 1.7 %collective-permute-start.30 = (bf16[128,1024]{1,0:T(8,128)(2,1)S(1)}, bf16[128,1024]{1,0:T(8,128)(2,1)S(1)}, u32[]{:S(2)}, u32[]{:S(2)}) collective-permute-start(bf16[128,1024]{1,0:T(8,128)(2,1)S(1)} %collective-permute-done.15.refs_7_), channel_id=1, source_target_pairs={{0,3},{1,0},{2,1},{3,2},{4,7},{5,4},{6,5},{7,6},{8,11},{9,8},{10,9... | collective-permute-start | bytes 786440 | tf_op jit(solution)/shard_map/ppermute | solution.py:310
  64.9 6.4 %chunk.6 = (f32[4,4,128,1024]{3,2,1,0:T(8,128)}, bf16[512,1024]{1,0:T(8,128)(2,1)S(1)}, bf16[512,3072]{1,0:T(8,128)(2,1)S(1)}) custom-call(s32[3]{0:T(128)S(1)} %get-tuple-element.28.refs_0_, f32[4,4]{1,0:T(4,128)S(1)} %copy-done, f32[4,1024]{1,0:T(4,128)S(1)} %multiply_exponential_fusion.1.refs_2_, f32[4,3072]{1,0:T(4,128)S(1)} %multiply_exponential_fusion.refs_3_, ...), custom_call_target="tpu_custom_call" | custom-call | flops 2147483648 | bytes 6291456 | tf_op jit(solution)/shard_map/chunk/pallas_call | solution.py:242
  71.7 6.5 %collective-permute-done.7.refs_4_ = bf16[128,1024]{1,0:T(8,128)(2,1)S(1)} collective-permute-done((bf16[128,1024]{1,0:T(8,128)(2,1)S(1)}, bf16[128,1024]{1,0:T(8,128)(2,1)S(1)}, u32[]{:S(2)}, u32[]{:S(2)}) %collective-permute-start.7) | collective-permute-done | bytes 262176 | tf_op jit(solution)/shard_map/ppermute | solution.py:310
  78.7 1.5 %collective-permute-start.29 = (bf16[128,1024]{1,0:T(8,128)(2,1)S(1)}, bf16[128,1024]{1,0:T(8,128)(2,1)S(1)}, u32[]{:S(2)}, u32[]{:S(2)}) collective-permute-start(bf16[128,1024]{1,0:T(8,128)(2,1)S(1)} %collective-permute-done.28.refs_7_), channel_id=1, source_target_pairs={{0,16},{16,0},{1,17},{17,1},{2,18},{18,2},{3,19},{19,3},{4,20},{20... | collective-permute-start | bytes 786440 | tf_op jit(solution)/shard_map/ppermute | solution.py:310
  80.2 3.6 %collective-permute-done.34.refs_5_ = bf16[128,1024]{1,0:T(8,128)(2,1)S(1)} collective-permute-done((bf16[128,1024]{1,0:T(8,128)(2,1)S(1)}, bf16[128,1024]{1,0:T(8,128)(2,1)S(1)}, u32[]{:S(2)}, u32[]{:S(2)}) %collective-permute-start.34) | collective-permute-done | bytes 262176 | tf_op jit(solution)/shard_map/ppermute | solution.py:310
  83.8 1.5 %collective-permute-start.32 = (bf16[128,1024]{1,0:T(8,128)(2,1)S(1)}, bf16[128,1024]{1,0:T(8,128)(2,1)S(1)}, u32[]{:S(2)}, u32[]{:S(2)}) collective-permute-start(bf16[128,1024]{1,0:T(8,128)(2,1)S(1)} %collective-permute-done.9.refs_9_), channel_id=1, source_target_pairs={{0,16},{16,0},{1,17},{17,1},{2,18},{18,2},{3,19},{19,3},{4,20},{20... | collective-permute-start | bytes 786440 | tf_op jit(solution)/shard_map/ppermute | solution.py:310
  85.9 9.3 %chunk.7.refs_14_ = f32[4,4,128,1024]{3,2,1,0:T(8,128)} custom-call(s32[4]{0:T(128)S(1)} %pad_add_fusion.7.refs_0_, f32[4,4]{1,0:T(4,128)S(1)} %copy-done, f32[4,1024]{1,0:T(4,128)S(1)} %multiply_exponential_fusion.1.refs_2_, f32[4,3072]{1,0:T(4,128)S(1)} %multiply_exponential_fusion.refs_3_, ...), custom_call_target="tpu_custom_call", output_to_operand_aliasing={{}: (12, {})} | custom-call | flops 4294967296 | bytes 8388608 | tf_op jit(solution)/shard_map/chunk/pallas_call | solution.py:242
  95.1 2.1 %collective-permute-start.21 = (bf16[128,1024]{1,0:T(8,128)(2,1)S(1)}, bf16[128,1024]{1,0:T(8,128)(2,1)S(1)}, u32[]{:S(2)}, u32[]{:S(2)}) collective-permute-start(bf16[128,1024]{1,0:T(8,128)(2,1)S(1)} %get-tuple-element.23.refs_6_), channel_id=1, source_target_pairs={{0,3},{1,0},{2,1},{3,2},{4,7},{5,4},{6,5},{7,6},{8,11},{9,8},{10,9... | collective-permute-start | bytes 786440 | tf_op jit(solution)/shard_map/ppermute | solution.py:310
  97.3 2.2 %collective-permute-start.10 = (bf16[128,1024]{1,0:T(8,128)(2,1)S(1)}, bf16[128,1024]{1,0:T(8,128)(2,1)S(1)}, u32[]{:S(2)}, u32[]{:S(2)}) collective-permute-start(bf16[128,1024]{1,0:T(8,128)(2,1)S(1)} %collective-permute-done.9.refs_9_), channel_id=1, source_target_pairs={{0,3},{1,0},{2,1},{3,2},{4,7},{5,4},{6,5},{7,6},{8,11},{9,8},{10,9... | collective-permute-start | bytes 786440 | tf_op jit(solution)/shard_map/ppermute | solution.py:310
  101.5 1.5 %collective-permute-start.25 = (bf16[128,1024]{1,0:T(8,128)(2,1)S(1)}, bf16[128,1024]{1,0:T(8,128)(2,1)S(1)}, u32[]{:S(2)}, u32[]{:S(2)}) collective-permute-start(bf16[128,1024]{1,0:T(8,128)(2,1)S(1)} %collective-permute-done.24.refs_6_), channel_id=1, source_target_pairs={{0,16},{16,0},{1,17},{17,1},{2,18},{18,2},{3,19},{19,3},{4,20},{20... | collective-permute-start | bytes 786440 | tf_op jit(solution)/shard_map/ppermute | solution.py:310
  103.0 9.2 %chunk.8.refs_10_ = f32[4,4,128,1024]{3,2,1,0:T(8,128)} custom-call(s32[4]{0:T(128)S(1)} %pad_add_fusion.5.refs_0_, f32[4,4]{1,0:T(4,128)S(1)} %copy-done, f32[4,1024]{1,0:T(4,128)S(1)} %multiply_exponential_fusion.1.refs_2_, f32[4,3072]{1,0:T(4,128)S(1)} %multiply_exponential_fusion.refs_3_, ...), custom_call_target="tpu_custom_call", output_to_operand_aliasing={{}: (14, {})} | custom-call | flops 4294967296 | bytes 8388608 | tf_op jit(solution)/shard_map/chunk/pallas_call | solution.py:242
  114.5 1.8 %collective-permute-start.8 = (bf16[128,1024]{1,0:T(8,128)(2,1)S(1)}, bf16[128,1024]{1,0:T(8,128)(2,1)S(1)}, u32[]{:S(2)}, u32[]{:S(2)}) collective-permute-start(bf16[128,1024]{1,0:T(8,128)(2,1)S(1)} %collective-permute-done.7.refs_4_), channel_id=1, source_target_pairs={{0,1},{1,2},{2,3},{3,0},{4,5},{5,6},{6,7},{7,4},{8,9},{9,10},{10,1... | collective-permute-start | bytes 786440 | tf_op jit(solution)/shard_map/ppermute | solution.py:310
  116.3 3.6 %collective-permute-done.25.refs_6_ = bf16[128,1024]{1,0:T(8,128)(2,1)S(1)} collective-permute-done((bf16[128,1024]{1,0:T(8,128)(2,1)S(1)}, bf16[128,1024]{1,0:T(8,128)(2,1)S(1)}, u32[]{:S(2)}, u32[]{:S(2)}) %collective-permute-start.25) | collective-permute-done | bytes 262176 | tf_op jit(solution)/shard_map/ppermute | solution.py:310
  119.9 1.5 %collective-permute-start.11 = (bf16[128,1024]{1,0:T(8,128)(2,1)S(1)}, bf16[128,1024]{1,0:T(8,128)(2,1)S(1)}, u32[]{:S(2)}, u32[]{:S(2)}) collective-permute-start(bf16[128,1024]{1,0:T(8,128)(2,1)S(1)} %collective-permute-done.10.refs_6_), channel_id=1, source_target_pairs={{0,16},{16,0},{1,17},{17,1},{2,18},{18,2},{3,19},{19,3},{4,20},{20... | collective-permute-start | bytes 786440 | tf_op jit(solution)/shard_map/ppermute | solution.py:310
  121.4 5.4 %chunk.9.refs_10_ = f32[4,4,128,1024]{3,2,1,0:T(8,128)} custom-call(s32[3]{0:T(128)S(1)} %get-tuple-element.21.refs_0_, f32[4,4]{1,0:T(4,128)S(1)} %copy-done, f32[4,1024]{1,0:T(4,128)S(1)} %multiply_exponential_fusion.1.refs_2_, f32[4,3072]{1,0:T(4,128)S(1)} %multiply_exponential_fusion.refs_3_, ...), custom_call_target="tpu_custom_call", output_to_operand_aliasing={{}: (10, {})} | custom-call | flops 2147483648 | bytes 6291456 | tf_op jit(solution)/shard_map/chunk/pallas_call | solution.py:242
  126.9 5.4 %chunk.10.refs_10_ = f32[4,4,128,1024]{3,2,1,0:T(8,128)} custom-call(s32[3]{0:T(128)S(1)} %get-tuple-element.27.refs_0_, f32[4,4]{1,0:T(4,128)S(1)} %copy-done, f32[4,1024]{1,0:T(4,128)S(1)} %multiply_exponential_fusion.1.refs_2_, f32[4,3072]{1,0:T(4,128)S(1)} %multiply_exponential_fusion.refs_3_, ...), custom_call_target="tpu_custom_call", output_to_operand_aliasing={{}: (10, {})} | custom-call | flops 2147483648 | bytes 6291456 | tf_op jit(solution)/shard_map/chunk/pallas_call | solution.py:242
  132.4 5.4 %chunk.11 = f32[4,4,128,1024]{3,2,1,0:T(8,128)} custom-call(s32[3]{0:T(128)S(1)} %get-tuple-element.29.refs_0_, f32[4,4]{1,0:T(4,128)S(1)} %copy-done, f32[4,1024]{1,0:T(4,128)S(1)} %multiply_exponential_fusion.1.refs_2_, f32[4,3072]{1,0:T(4,128)S(1)} %multiply_exponential_fusion.refs_3_, ...), custom_call_target="tpu_custom_call", output_to_operand_aliasing={{}: (10, {})} | custom-call | flops 2147483648 | bytes 6291456 | tf_op jit(solution)/shard_map/chunk/pallas_call | solution.py:242
  (62 shorter events, 14.5 us)
Async XLA Ops:
  1.3 22.6 %collective-permute-start.3 = (bf16[128,1024]{1,0:T(8,128)(2,1)S(1)}, bf16[128,1024]{1,0:T(8,128)(2,1)S(1)}, u32[]{:S(2)}, u32[]{:S(2)}) collective-permute-start(bf16[128,1024]{1,0:T(8,128)(2,1)S(1)} %get-tuple-element.24.refs_4_), channel_id=1, source_target_pairs={{0,2},{1,3},{2,0},{3,1},{4,6},{5,7},{6,4},{7,5},{8,10},{9,11},{10,... | collective-permute-start | bytes 786440 | tf_op jit(solution)/shard_map/ppermute | solution.py:310
  5.5 20.2 %collective-permute-start.14 = (bf16[128,1024]{1,0:T(8,128)(2,1)S(1)}, bf16[128,1024]{1,0:T(8,128)(2,1)S(1)}, u32[]{:S(2)}, u32[]{:S(2)}) collective-permute-start(bf16[128,1024]{1,0:T(8,128)(2,1)S(1)} %get-tuple-element.23.refs_6_), channel_id=1, source_target_pairs={{0,1},{1,2},{2,3},{3,0},{4,5},{5,6},{6,7},{7,4},{8,9},{9,10},{10,1... | collective-permute-start | bytes 786440 | tf_op jit(solution)/shard_map/ppermute | solution.py:310
  7.1 18.7 %collective-permute-start.15 = (bf16[128,1024]{1,0:T(8,128)(2,1)S(1)}, bf16[128,1024]{1,0:T(8,128)(2,1)S(1)}, u32[]{:S(2)}, u32[]{:S(2)}) collective-permute-start(bf16[128,1024]{1,0:T(8,128)(2,1)S(1)} %get-tuple-element.25.refs_4_), channel_id=1, source_target_pairs={{0,3},{1,0},{2,1},{3,2},{4,7},{5,4},{6,5},{7,6},{8,11},{9,8},{10,9... | collective-permute-start | bytes 786440 | tf_op jit(solution)/shard_map/ppermute | solution.py:310
  23.9 13.6 %collective-permute-start.4 = (bf16[128,1024]{1,0:T(8,128)(2,1)S(1)}, bf16[128,1024]{1,0:T(8,128)(2,1)}, u32[]{:S(2)}, u32[]{:S(2)}) collective-permute-start(bf16[128,1024]{1,0:T(8,128)(2,1)S(1)} %collective-permute-done.3.refs_6_), channel_id=1, source_target_pairs={{0,8},{4,12},{8,0},{12,4},{1,9},{5,13},{9,1},{13,5},{2,10},{6,14},... | collective-permute-start | bytes 786440 | tf_op jit(solution)/shard_map/ppermute | solution.py:310
  26.7 20.7 %collective-permute-start.18 = (bf16[384,1024]{1,0:T(8,128)(2,1)}, bf16[384,1024]{1,0:T(8,128)(2,1)S(1)}, u32[]{:S(2)}, u32[]{:S(2)}) collective-permute-start(bf16[384,1024]{1,0:T(8,128)(2,1)} %pad_maximum_fusion), channel_id=1, source_target_pairs={{0,8},{4,12},{8,0},{12,4},{1,9},{5,13},{9,1},{13,5},{2,10},{6,14},... | collective-permute-start | bytes 2359304 | tf_op jit(solution)/shard_map/ppermute | solution.py:310
  27.8 9.8 %collective-permute-start = (f32[1,1152]{1,0:T(1,128)S(1)}, f32[1,1152]{1,0:T(1,128)S(1)}, u32[]{:S(2)}, u32[]{:S(2)}) collective-permute-start(f32[1,1152]{1,0:T(1,128)S(1)} %broadcast_in_dim.9), channel_id=1, source_target_pairs={{0,1},{1,2},{2,3},{3,0},{4,5},{5,6},{6,7},{7,4},{8,9},{9,10},{10,1... | collective-permute-start | bytes 13832 | tf_op jit(solution)/shard_map/ppermute | solution.py:310
  34.5 6.9 %collective-permute-start.2 = (f32[1,1152]{1,0:T(1,128)S(1)}, f32[1,1152]{1,0:T(1,128)S(1)}, u32[]{:S(2)}, u32[]{:S(2)}) collective-permute-start(f32[1,1152]{1,0:T(1,128)S(1)} %broadcast_in_dim.9), channel_id=1, source_target_pairs={{0,3},{1,0},{2,1},{3,2},{4,7},{5,4},{6,5},{7,6},{8,11},{9,8},{10,9... | collective-permute-start | bytes 13832 | tf_op jit(solution)/shard_map/ppermute | solution.py:310
  37.6 11.0 %collective-permute-start.28 = (bf16[128,1024]{1,0:T(8,128)(2,1)S(1)}, bf16[128,1024]{1,0:T(8,128)(2,1)S(1)}, u32[]{:S(2)}, u32[]{:S(2)}) collective-permute-start(bf16[128,1024]{1,0:T(8,128)(2,1)S(1)} %get-tuple-element.24.refs_4_), channel_id=1, source_target_pairs={{0,1},{1,2},{2,3},{3,0},{4,5},{5,6},{6,7},{7,4},{8,9},{9,10},{10,1... | collective-permute-start | bytes 786440 | tf_op jit(solution)/shard_map/ppermute | solution.py:310
  37.6 14.4 %collective-permute-start.9 = (bf16[128,1024]{1,0:T(8,128)(2,1)S(1)}, bf16[128,1024]{1,0:T(8,128)(2,1)S(1)}, u32[]{:S(2)}, u32[]{:S(2)}) collective-permute-start(bf16[128,1024]{1,0:T(8,128)(2,1)S(1)} %get-tuple-element.26.refs_4_), channel_id=1, source_target_pairs={{0,3},{1,0},{2,1},{3,2},{4,7},{5,4},{6,5},{7,6},{8,11},{9,8},{10,9... | collective-permute-start | bytes 786440 | tf_op jit(solution)/shard_map/ppermute | solution.py:310
  41.4 12.1 %collective-permute-start.12 = (bf16[128,1024]{1,0:T(8,128)(2,1)S(1)}, bf16[128,1024]{1,0:T(8,128)(2,1)S(1)}, u32[]{:S(2)}, u32[]{:S(2)}) collective-permute-start(bf16[128,1024]{1,0:T(8,128)(2,1)S(1)} %get-tuple-element.23.refs_6_), channel_id=1, source_target_pairs={{0,16},{16,0},{1,17},{17,1},{2,18},{18,2},{3,19},{19,3},{4,20},{20... | collective-permute-start | bytes 786440 | tf_op jit(solution)/shard_map/ppermute | solution.py:310
  43.1 18.8 %collective-permute-start.16 = (bf16[384,1024]{1,0:T(8,128)(2,1)}, bf16[384,1024]{1,0:T(8,128)(2,1)}, u32[]{:S(2)}, u32[]{:S(2)}) collective-permute-start(bf16[384,1024]{1,0:T(8,128)(2,1)} %pad_maximum_fusion), channel_id=1, source_target_pairs={{0,4},{4,0},{8,12},{12,8},{1,5},{5,1},{9,13},{13,9},{2,6},{6,2},{1... | collective-permute-start | bytes 2359304 | tf_op jit(solution)/shard_map/ppermute | solution.py:310
  47.4 16.2 %collective-permute-start.19 = (bf16[384,1024]{1,0:T(8,128)(2,1)S(1)}, bf16[384,1024]{1,0:T(8,128)(2,1)S(1)}, u32[]{:S(2)}, u32[]{:S(2)}) collective-permute-start(bf16[384,1024]{1,0:T(8,128)(2,1)S(1)} %collective-permute-done.18.refs_10_), channel_id=1, source_target_pairs={{0,4},{4,0},{8,12},{12,8},{1,5},{5,1},{9,13},{13,9},{2,6},{6,2},{1... | collective-permute-start | bytes 2359304 | tf_op jit(solution)/shard_map/ppermute | solution.py:310
  48.6 10.7 %collective-permute-start.22 = (bf16[128,1024]{1,0:T(8,128)(2,1)S(1)}, bf16[128,1024]{1,0:T(8,128)(2,1)S(1)}, u32[]{:S(2)}, u32[]{:S(2)}) collective-permute-start(bf16[128,1024]{1,0:T(8,128)(2,1)S(1)} %get-tuple-element.26.refs_4_), channel_id=1, source_target_pairs={{0,1},{1,2},{2,3},{3,0},{4,5},{5,6},{6,7},{7,4},{8,9},{9,10},{10,1... | collective-permute-start | bytes 786440 | tf_op jit(solution)/shard_map/ppermute | solution.py:310
  52.0 33.4 %collective-permute-start.33 = (bf16[384,1024]{1,0:T(8,128)(2,1)}, bf16[384,1024]{1,0:T(8,128)(2,1)S(1)}, u32[]{:S(2)}, u32[]{:S(2)}) collective-permute-start(bf16[384,1024]{1,0:T(8,128)(2,1)} %pad_maximum_fusion), channel_id=1, source_target_pairs={{0,16},{16,0},{1,17},{17,1},{2,18},{18,2},{3,19},{19,3},{4,20},{20... | collective-permute-start | bytes 2359304 | tf_op jit(solution)/shard_map/ppermute | solution.py:310
  59.4 12.0 %collective-permute-start.26 = (bf16[128,1024]{1,0:T(8,128)(2,1)S(1)}, bf16[128,1024]{1,0:T(8,128)(2,1)S(1)}, u32[]{:S(2)}, u32[]{:S(2)}) collective-permute-start(bf16[128,1024]{1,0:T(8,128)(2,1)S(1)} %get-tuple-element.24.refs_4_), channel_id=1, source_target_pairs={{0,3},{1,0},{2,1},{3,2},{4,7},{5,4},{6,5},{7,6},{8,11},{9,8},{10,9... | collective-permute-start | bytes 786440 | tf_op jit(solution)/shard_map/ppermute | solution.py:310
  60.3 17.9 %collective-permute-start.7 = (bf16[128,1024]{1,0:T(8,128)(2,1)S(1)}, bf16[128,1024]{1,0:T(8,128)(2,1)S(1)}, u32[]{:S(2)}, u32[]{:S(2)}) collective-permute-start(bf16[128,1024]{1,0:T(8,128)(2,1)S(1)} %get-tuple-element.25.refs_4_), channel_id=1, source_target_pairs={{0,16},{16,0},{1,17},{17,1},{2,18},{18,2},{3,19},{19,3},{4,20},{20... | collective-permute-start | bytes 786440 | tf_op jit(solution)/shard_map/ppermute | solution.py:310
  61.9 16.8 %collective-permute-start.30 = (bf16[128,1024]{1,0:T(8,128)(2,1)S(1)}, bf16[128,1024]{1,0:T(8,128)(2,1)S(1)}, u32[]{:S(2)}, u32[]{:S(2)}) collective-permute-start(bf16[128,1024]{1,0:T(8,128)(2,1)S(1)} %collective-permute-done.15.refs_7_), channel_id=1, source_target_pairs={{0,3},{1,0},{2,1},{3,2},{4,7},{5,4},{6,5},{7,6},{8,11},{9,8},{10,9... | collective-permute-start | bytes 786440 | tf_op jit(solution)/shard_map/ppermute | solution.py:310
  63.6 20.2 %collective-permute-start.34 = (bf16[128,1024]{1,0:T(8,128)(2,1)S(1)}, bf16[128,1024]{1,0:T(8,128)(2,1)S(1)}, u32[]{:S(2)}, u32[]{:S(2)}) collective-permute-start(bf16[128,1024]{1,0:T(8,128)(2,1)S(1)} %collective-permute-done.3.refs_6_), channel_id=1, source_target_pairs={{0,16},{16,0},{1,17},{17,1},{2,18},{18,2},{3,19},{19,3},{4,20},{20... | collective-permute-start | bytes 786440 | tf_op jit(solution)/shard_map/ppermute | solution.py:310
  71.3 23.8 %collective-permute-start.20 = (bf16[128,1024]{1,0:T(8,128)(2,1)S(1)}, bf16[128,1024]{1,0:T(8,128)(2,1)S(1)}, u32[]{:S(2)}, u32[]{:S(2)}) collective-permute-start(bf16[128,1024]{1,0:T(8,128)(2,1)S(1)} %get-tuple-element.25.refs_4_), channel_id=1, source_target_pairs={{0,1},{1,2},{2,3},{3,0},{4,5},{5,6},{6,7},{7,4},{8,9},{9,10},{10,1... | collective-permute-start | bytes 786440 | tf_op jit(solution)/shard_map/ppermute | solution.py:310
  78.2 19.0 %collective-permute-start.24 = (bf16[128,1024]{1,0:T(8,128)(2,1)S(1)}, bf16[128,1024]{1,0:T(8,128)(2,1)S(1)}, u32[]{:S(2)}, u32[]{:S(2)}) collective-permute-start(bf16[128,1024]{1,0:T(8,128)(2,1)S(1)} %collective-permute-done.14.refs_5_), channel_id=1, source_target_pairs={{0,1},{1,2},{2,3},{3,0},{4,5},{5,6},{6,7},{7,4},{8,9},{9,10},{10,1... | collective-permute-start | bytes 786440 | tf_op jit(solution)/shard_map/ppermute | solution.py:310
  78.7 20.8 %collective-permute-start.29 = (bf16[128,1024]{1,0:T(8,128)(2,1)S(1)}, bf16[128,1024]{1,0:T(8,128)(2,1)S(1)}, u32[]{:S(2)}, u32[]{:S(2)}) collective-permute-start(bf16[128,1024]{1,0:T(8,128)(2,1)S(1)} %collective-permute-done.28.refs_7_), channel_id=1, source_target_pairs={{0,16},{16,0},{1,17},{17,1},{2,18},{18,2},{3,19},{19,3},{4,20},{20... | collective-permute-start | bytes 786440 | tf_op jit(solution)/shard_map/ppermute | solution.py:310
  83.8 17.2 %collective-permute-start.32 = (bf16[128,1024]{1,0:T(8,128)(2,1)S(1)}, bf16[128,1024]{1,0:T(8,128)(2,1)S(1)}, u32[]{:S(2)}, u32[]{:S(2)}) collective-permute-start(bf16[128,1024]{1,0:T(8,128)(2,1)S(1)} %collective-permute-done.9.refs_9_), channel_id=1, source_target_pairs={{0,16},{16,0},{1,17},{17,1},{2,18},{18,2},{3,19},{19,3},{4,20},{20... | collective-permute-start | bytes 786440 | tf_op jit(solution)/shard_map/ppermute | solution.py:310
  85.4 16.1 %collective-permute-start.31 = (bf16[128,1024]{1,0:T(8,128)(2,1)S(1)}, bf16[128,1024]{1,0:T(8,128)(2,1)S(1)}, u32[]{:S(2)}, u32[]{:S(2)}) collective-permute-start(bf16[128,1024]{1,0:T(8,128)(2,1)S(1)} %collective-permute-done.30.refs_8_), channel_id=1, source_target_pairs={{0,16},{16,0},{1,17},{17,1},{2,18},{18,2},{3,19},{19,3},{4,20},{20... | collective-permute-start | bytes 786440 | tf_op jit(solution)/shard_map/ppermute | solution.py:310
  95.1 31.7 %collective-permute-start.21 = (bf16[128,1024]{1,0:T(8,128)(2,1)S(1)}, bf16[128,1024]{1,0:T(8,128)(2,1)S(1)}, u32[]{:S(2)}, u32[]{:S(2)}) collective-permute-start(bf16[128,1024]{1,0:T(8,128)(2,1)S(1)} %get-tuple-element.23.refs_6_), channel_id=1, source_target_pairs={{0,3},{1,0},{2,1},{3,2},{4,7},{5,4},{6,5},{7,6},{8,11},{9,8},{10,9... | collective-permute-start | bytes 786440 | tf_op jit(solution)/shard_map/ppermute | solution.py:310
  97.3 17.3 %collective-permute-start.10 = (bf16[128,1024]{1,0:T(8,128)(2,1)S(1)}, bf16[128,1024]{1,0:T(8,128)(2,1)S(1)}, u32[]{:S(2)}, u32[]{:S(2)}) collective-permute-start(bf16[128,1024]{1,0:T(8,128)(2,1)S(1)} %collective-permute-done.9.refs_9_), channel_id=1, source_target_pairs={{0,3},{1,0},{2,1},{3,2},{4,7},{5,4},{6,5},{7,6},{8,11},{9,8},{10,9... | collective-permute-start | bytes 786440 | tf_op jit(solution)/shard_map/ppermute | solution.py:310
  99.5 12.8 %collective-permute-start.23 = (bf16[128,1024]{1,0:T(8,128)(2,1)S(1)}, bf16[128,1024]{1,0:T(8,128)(2,1)S(1)}, u32[]{:S(2)}, u32[]{:S(2)}) collective-permute-start(bf16[128,1024]{1,0:T(8,128)(2,1)S(1)} %collective-permute-done.22.refs_5_), channel_id=1, source_target_pairs={{0,16},{16,0},{1,17},{17,1},{2,18},{18,2},{3,19},{19,3},{4,20},{20... | collective-permute-start | bytes 786440 | tf_op jit(solution)/shard_map/ppermute | solution.py:310
  101.0 13.3 %collective-permute-start.27 = (bf16[128,1024]{1,0:T(8,128)(2,1)S(1)}, bf16[128,1024]{1,0:T(8,128)(2,1)S(1)}, u32[]{:S(2)}, u32[]{:S(2)}) collective-permute-start(bf16[128,1024]{1,0:T(8,128)(2,1)S(1)} %collective-permute-done.26.refs_7_), channel_id=1, source_target_pairs={{0,16},{16,0},{1,17},{17,1},{2,18},{18,2},{3,19},{19,3},{4,20},{20... | collective-permute-start | bytes 786440 | tf_op jit(solution)/shard_map/ppermute | solution.py:310
  101.5 18.4 %collective-permute-start.25 = (bf16[128,1024]{1,0:T(8,128)(2,1)S(1)}, bf16[128,1024]{1,0:T(8,128)(2,1)S(1)}, u32[]{:S(2)}, u32[]{:S(2)}) collective-permute-start(bf16[128,1024]{1,0:T(8,128)(2,1)S(1)} %collective-permute-done.24.refs_6_), channel_id=1, source_target_pairs={{0,16},{16,0},{1,17},{17,1},{2,18},{18,2},{3,19},{19,3},{4,20},{20... | collective-permute-start | bytes 786440 | tf_op jit(solution)/shard_map/ppermute | solution.py:310
  112.3 20.0 %collective-permute-start.6 = (bf16[128,1024]{1,0:T(8,128)(2,1)S(1)}, bf16[128,1024]{1,0:T(8,128)(2,1)S(1)}, u32[]{:S(2)}, u32[]{:S(2)}) collective-permute-start(bf16[128,1024]{1,0:T(8,128)(2,1)S(1)} %get-tuple-element.24.refs_4_), channel_id=1, source_target_pairs={{0,16},{16,0},{1,17},{17,1},{2,18},{18,2},{3,19},{19,3},{4,20},{20... | collective-permute-start | bytes 786440 | tf_op jit(solution)/shard_map/ppermute | solution.py:310
  114.3 18.1 %collective-permute-start.13 = (bf16[128,1024]{1,0:T(8,128)(2,1)S(1)}, bf16[128,1024]{1,0:T(8,128)(2,1)S(1)}, u32[]{:S(2)}, u32[]{:S(2)}) collective-permute-start(bf16[128,1024]{1,0:T(8,128)(2,1)S(1)} %collective-permute-done.12.refs_8_), channel_id=1, source_target_pairs={{0,3},{1,0},{2,1},{3,2},{4,7},{5,4},{6,5},{7,6},{8,11},{9,8},{10,9... | collective-permute-start | bytes 786440 | tf_op jit(solution)/shard_map/ppermute | solution.py:310
  114.5 17.8 %collective-permute-start.8 = (bf16[128,1024]{1,0:T(8,128)(2,1)S(1)}, bf16[128,1024]{1,0:T(8,128)(2,1)S(1)}, u32[]{:S(2)}, u32[]{:S(2)}) collective-permute-start(bf16[128,1024]{1,0:T(8,128)(2,1)S(1)} %collective-permute-done.7.refs_4_), channel_id=1, source_target_pairs={{0,1},{1,2},{2,3},{3,0},{4,5},{5,6},{6,7},{7,4},{8,9},{9,10},{10,1... | collective-permute-start | bytes 786440 | tf_op jit(solution)/shard_map/ppermute | solution.py:310
  119.9 12.5 %collective-permute-start.11 = (bf16[128,1024]{1,0:T(8,128)(2,1)S(1)}, bf16[128,1024]{1,0:T(8,128)(2,1)S(1)}, u32[]{:S(2)}, u32[]{:S(2)}) collective-permute-start(bf16[128,1024]{1,0:T(8,128)(2,1)S(1)} %collective-permute-done.10.refs_6_), channel_id=1, source_target_pairs={{0,16},{16,0},{1,17},{17,1},{2,18},{18,2},{3,19},{19,3},{4,20},{20... | collective-permute-start | bytes 786440 | tf_op jit(solution)/shard_map/ppermute | solution.py:310
  (4 other events, 18.2 us)

commit v3 on v2

--- a/solution.py
+++ b/solution.py
@@ -16,86 +16,101 @@
     near = sorted(range(1, n), key=lambda k: (min(k, n - k), k))
     late = [m for pair in zip(range(1, n), range(n - 1, 0, -1)) for m in pair]
     late = list(dict.fromkeys(late))
-    ends = near[:2]
-    groups = [[0, *ends]] + [[k] for k in near[2:]]
-
-    def emit(axis, shift, source, target):
-        if target not in known:
-            known.add(target)
-            plan.append(("move", axis, shift, source, target))
-
-    def direct(m, k):
-        return m == 0 or k in ends
-
-    def own(m, k, dy=None):
-        at = (lambda *key: ("Y", dy, *key)) if dy else (lambda *key: ("P", *key))
-        start = (lambda d: ("Y", dy, d, 0)) if dy else (lambda d: ("S", d))
-        if direct(m, k):
-            shift = k if 2 * k <= n else k - n
-            emit("tm", shift, start((k + m) % n), at(m, k))
-        elif 2 * k < n or (2 * k == n and 2 * m > n):
-            own((m + 1) % n, k - 1, dy)
-            emit("tm", 1, at((m + 1) % n, k - 1), at(m, k))
-        else:
-            own(m - 1, k + 1, dy)
-            emit("tm", -1, at(m - 1, k + 1), at(m, k))
-
-    def across(m, ks):
-        for dy in range(1, rows):
-            for k in ks:
-                emit("row", dy, ("P", m, k) if k else ("S", m), ("Y", dy, m, k))
-
-    def spread(g, ds):
+    last = late[-1]
+    ends, rest = near[:2], near[2:]
+    even, odd = range(2, cols, 2), range(3, cols, 2)
+    others = range(1, rows)
+
+    def move(axis, shift, sources, gives):
+        if gives[0] not in known:
+            known.update(gives)
+            plan.append(("move", axis, shift, tuple(sources), tuple(gives)))
+
+    def straight(k, stages, dys=(0,)):
+        shift = k if 2 * k <= n else k - n
+        pairs = [(m, dy) for dy in dys for m in stages]
+        move(
+            "tm",
+            shift,
+            [("Y", dy, (k + m) % n, 0) if dy else ("S", (k + m) % n) for m, dy in pairs],
+            [("Y", dy, m, k) if dy else ("P", m, k) for m, dy in pairs],
+        )
+
+    def relay(m, k):
+        if ("P", m, k) in known:
+            return
+        ahead = 2 * k < n or (2 * k == n and 2 * m > n)
+        source = ((m + 1) % n, k - 1) if ahead else (m - 1, k + 1)
+        if source[0] and source[1] in rest:
+            relay(*source)
+        move("tm", 1 if ahead else -1, [("P", *source)], [("P", m, k)])
+
+    def across(pieces):
+        for dy in others:
+            move("row", dy, [("P", *p) for p in pieces], [("Y", dy, *p) for p in pieces])
+
+    def spread(ks, ds):
         for d in ds:
-            if d & 1 and d > 1:
-                emit("col", 1, ("F", d - 1, g), ("F", d, g))
-            else:
-                emit("col", d, ("F", 0, g), ("F", d, g))
+            low = d & 1 if d > 1 else 0
+            sources = [("F", d - low, k) if low else ("P", 0, k) for k in ks]
+            move("col", low or d, sources, [("F", d, k) for k in ks])
 
     def kernel(*chunks):
         plan.append(("kernel", chunks))
 
-    even, odd = range(2, cols, 2), range(3, cols, 2)
-    others = range(1, rows)
     for k in near:
-        own(0, k)
-    for m in late:
-        across(m, [0])
-    for k in ends:
-        own(late[0], k)
+        straight(k, [0])
+    spread([0], even)
+    across([(late[0], 0)])
     for k in near:
-        plan.append(("move", "tm", k, ("D", 0), ("D", k)))
-    for g in range(len(groups)):
-        spread(g, even)
-        for dy in others:
-            emit("row", dy, ("F", 0, g), ("Y", dy, "F", g))
-        spread(g, [1] if cols > 1 else [])
-        if g == 0:
-            for m in late[:2]:
-                for k in near:
-                    own(m, k)
-    for g in range(len(groups)):
-        spread(g, odd)
-    last = late[-1]
+        plan.append(("move", "tm", k, (("D", 0),), (("D", k),)))
+    spread([0], [1][: cols - 1])
+    for m in late[1:]:
+        across([(m, 0)])
+    for k in ends:
+        spread([k], even)
+    for k in ends:
+        spread([k], [1][: cols - 1])
+    for k in ends:
+        straight(k, [late[0]])
+    across([(0, k) for k in [0, *ends]])
+    for k in rest:
+        spread([k], even)
+        spread([k], [1][: cols - 1])
+    for k in rest:
+        relay(late[0], k)
+    for k in ends:
+        straight(k, [late[1]])
+    for k in rest:
+        relay(late[1], k)
+    for k in rest:
+        across([(0, k)])
+    for k in [0, *near]:
+        spread([k], odd)
+    for k in ends:
+        across([(late[0], k)])
     kernel((0, 0))
-    across(late[0], near)
+    for k in rest:
+        across([(late[0], k)])
     for m in late[2:]:
-        for k in reversed(near):
-            own(m, k)
-    kernel(*[(dy, 0) for dy in others], (0, late[0]))
-    for dy in others:
-        for k in ends:
-            own(last, k, dy)
+        for k in rest:
+            relay(m, k)
+        if m != last:
+            for k in ends:
+                straight(k, [m])
+    for k in ends:
+        straight(k, [last], [0, *others])
+    kernel(*[(dy, 0) for dy in others])
     for m in late[1:-1]:
-        across(m, near)
-    kernel((0, late[1]), *[(dy, late[0]) for dy in others])
-    across(last, [k for k in near if k not in ends])
-    for m in late[1:-1]:
-        kernel(*[(dy, m) for dy in others])
-    for m in late[2:]:
-        kernel((0, m))
-    kernel(*[(dy, last) for dy in others])
-    return plan, groups
+        for k in near:
+            across([(m, k)])
+        if m == late[1]:
+            kernel(*[(dy, late[0]) for dy in [0, *others]])
+    for k in rest:
+        across([(last, k)])
+    for m in late[1:]:
+        kernel(*[(dy, m) for dy in [0, *others]])
+    return plan
 
 
 def chunk_kernel(chunks, blocks, count, *refs):
@@ -114,6 +129,7 @@
     bo, be = co.shape[2] // count, ce.shape[2] // count
     width = co.shape[1]
     cols = fo.shape[0] // width
+    column, z = place[0], place[1]
 
     def pair(piece, into_o, into_e, sem, i):
         source, there, start, size, at = piece
@@ -156,7 +172,6 @@
 
     step, tall = 16, 64
     contract = (((1,), (1,)), ((), ()))
-    column, z = place[0], place[1]
     weights = [
         [-cosines[f, lax.rem(z + times - t, times)] for t in range(times)] for f in range(freqs)
     ]
@@ -270,7 +285,7 @@
     )(*operands)
 
 
-def streamed(plan, groups, sizes, filled, empty, filled_depth, empty_depth, time_points, cosines):
+def streamed(plan, sizes, filled, empty, filled_depth, empty_depth, time_points, cosines):
     n, rows, cols = sizes["tm"], sizes["row"], sizes["col"]
     z, r, c = lax.axis_index("tm"), lax.axis_index("row"), lax.axis_index("col")
     points, bo = filled.shape[1:]
@@ -278,40 +293,53 @@
     width = points // n
     shape = (cosines.shape[0], cols, width, rows * points)
     whole = jnp.concatenate([filled[0], empty[0]], axis=1)
-    values = {}
+    held, joined = {}, {}
     for d in range(n):
-        values["S", d] = lax.dynamic_slice_in_dim(whole, lax.rem(z + d, n) * width, width, 0)
+        own = lax.dynamic_slice_in_dim(whole, lax.rem(z + d, n) * width, width, 0)
+        held["S", d] = held["P", d, 0] = (own, 0)
     depth = jnp.concatenate([filled_depth, empty_depth]).astype(jnp.float32)
-    values["D", 0] = jnp.concatenate([depth, jnp.broadcast_to(time_points, (LANES,))])[None, :]
+    depth = jnp.concatenate([depth, jnp.broadcast_to(time_points, (LANES,))])[None, :]
+    held["D", 0] = (depth, 0)
     perms = {
         "tm": lambda s: [(i, (i + s) % n) for i in range(n)],
         "row": lambda s: [(i, (i + s) % rows) for i in range(rows)],
         "col": lambda s: [(i, i ^ s) for i in range(cols)],
     }
-    home = {k: (g, i) for g, group in enumerate(groups) for i, k in enumerate(group)}
-
-    def lookup(key):
-        if key not in values and key[0] == "F" and key[1] == 0:
-            parts = [values["P", 0, k] if k else values["S", 0] for k in groups[key[2]]]
-            values[key] = parts[0] if len(parts) == 1 else jnp.concatenate(parts, axis=0)
-        return values[key]
-
-    def find(dy, m, k):
-        if dy and m == 0:
-            return lookup(("Y", dy, "F", home[k][0])), home[k][1] * width
-        if dy:
-            return lookup(("Y", dy, m, k)), 0
-        return lookup(("P", m, k) if k else ("S", m)), 0
-
-    scales = kept = out = None
+
+    result = [None]
+
+    def after(array):
+        if result[0] is not None:
+            array, result[0] = lax.optimization_barrier((array, result[0]))
+        return array
+
+    def join(keys):
+        if keys not in joined:
+            array, _ = held[keys[0]]
+            spots = [held[key] for key in keys]
+            in_place = [spot[0] is array and spot[1] == i * width for i, spot in enumerate(spots)]
+            if all(in_place) and array.shape[0] <= len(keys) * width:
+                joined[keys] = array
+            else:
+                parts = [
+                    a if a.shape[0] == width else lax.slice_in_dim(after(a), at, at + width)
+                    for a, at in spots
+                ]
+                joined[keys] = parts[0] if len(parts) == 1 else jnp.concatenate(parts, axis=0)
+        return joined[keys]
+
+    scales = kept = None
     for step in plan:
         if step[0] == "move":
-            _, axis, shift, source, target = step
-            values[target] = lax.ppermute(lookup(source), axis, perms[axis](shift))
+            _, axis, shift, keys, gives = step
+            moved = lax.ppermute(join(keys), axis, perms[axis](shift))
+            for at, key in enumerate(gives):
+                held[key] = (moved, at * width)
             continue
         sources = []
 
-        def entry(array, there, row, k):
+        def entry(key, row, k):
+            array, there = held[key]
             for at, other in enumerate(sources):
                 if other is array:
                     return (at, there, row, width, k)
@@ -320,36 +348,41 @@
 
         blocks = []
         if scales is None:
-            held = [values["D", k] for k in range(n)]
-            end = ("F", cols - 1, len(groups) - 1)
-            *held, values[end] = lax.optimization_barrier((*held, lookup(end)))
-            stacked = jnp.concatenate(held, axis=0)
+            stacked = [held["D", k][0] for k in range(n)]
+            end = ("F", cols - 1, n // 2)
+            *stacked, array = lax.optimization_barrier((*stacked, held[end][0]))
+            held[end] = (array, held[end][1])
+            stacked = jnp.concatenate(stacked, axis=0)
             deep, tau = stacked[:, : bo + be], stacked[:, bo + be :][:, :1]
             scales = [
                 jnp.exp(-piece.reshape(1, -1) * tau) for piece in (deep[:, :bo], deep[:, bo:])
             ]
             for d in range(cols):
                 for k in range(n):
-                    g, at = home[k]
-                    if d:
-                        blocks.append(
-                            entry(lookup(("F", d, g)), at * width, d * width, k)
-                        )
-                    else:
-                        blocks.append(entry(*find(0, 0, k), 0, k))
+                    key = ("F", d, k) if d else ("P", 0, k)
+                    blocks.append(entry(key, d * width, k))
         chunks, spots = [], []
         for dy, m in step[1]:
-            chunks.append(tuple(entry(*find(dy, m, k), 0, k) for k in range(n)))
+            keys = [("Y", dy, m, k) if dy else ("P", m, k) for k in range(n)]
+            chunks.append(tuple(entry(key, 0, k) for k, key in enumerate(keys)))
             spots.append(lax.rem(r + rows - dy, rows) * n + lax.rem(z + m, n))
         place = jnp.stack([c, z, *spots]).astype(jnp.int32)
-        result = chunk_call(
-            place, cosines, scales, sources, tuple(chunks), tuple(blocks), kept, out, shape, n
+        done = chunk_call(
+            place,
+            cosines,
+            scales,
+            sources,
+            tuple(chunks),
+            tuple(blocks),
+            kept,
+            result[0],
+            shape,
+            n,
         )
         if blocks:
-            out, *kept = result
-        else:
-            out = result
-    return out
+            done, *kept = done
+        result[0] = done
+    return result[0]
 
 
 def gathered(sizes, filled, empty, filled_depth, empty_depth, time_points, cosines):
@@ -388,13 +421,13 @@
     sizes = dict(mesh.shape)
     in_specs = (P("col", "row", "tm"), P("col", "row", "tm"), P("tm"), P("tm"), P("tm"), P())
     out_specs = P(None, None, ("row", "tm"), "col")
-    plan, groups = make_plan(sizes["tm"], sizes["row"], sizes["col"])
+    plan = make_plan(sizes["tm"], sizes["row"], sizes["col"])
 
     def on_device(filled, *rest):
         width = filled.shape[1] // sizes["tm"]
-        if width % LANES or sizes["col"] & (sizes["col"] - 1):
+        if width % LANES or sizes["tm"] % 2 or sizes["tm"] < 4 or sizes["col"] not in (2, 4):
             return gathered(sizes, filled, *rest)
-        return streamed(plan, groups, sizes, filled, *rest)
+        return streamed(plan, sizes, filled, *rest)
 
     return jax.shard_map(
         on_device, mesh=mesh, in_specs=in_specs, out_specs=out_specs, check_vma=False

time: 138 us -> 151 us (1.094)
  waiting for transfers between devices: 42.2 us -> 58.7 us
  starting transfers between devices: 49.1 us -> 42.8 us
  local copies, waits for them, and re-layouts: 0.7 us -> 2.64 us
  other arithmetic: 3.6 us -> 5.31 us
    ppermute x35 -> x39, waiting for transfers between devices: 42.2 us -> 58.7 us  [streamed(): moved = lax.ppermute(join(keys), axis, perms[axis](shift))]
    ppermute x35 -> x39, starting transfers between devices: 49.1 us -> 42.8 us  [streamed(): moved = lax.ppermute(join(keys), axis, perms[axis](shift))]
    unnamed x3 -> x15, local copies, waits for them, and re-layouts: 0.68 us -> 2.62 us
    concatenate x1 -> x3, other arithmetic: 0.94 us -> 2.64 us  [join(): jnp.concatenate(parts, axis=0)]
    pallas_call x6 -> x5, Pallas kernels: 41.3 us -> 39.8 us  [chunk_call(): pl.pallas_call(functools.partial(chunk_kernel, chunks, blocks, count), ou...]
  transfers between devices with their start and end apart: 35 -> 39, of which waited for: 9 -> 12; matrix products, arithmetic and copies ran while one was open for 2% -> 3% of each run, Pallas kernels for 26% -> 20%
where the time goes in v3:
time: 151 us; the launch traced here: 150 us
  waiting for transfers between devices  58.7 us (39%)
  starting transfers between devices  42.8 us (28%)
  Pallas kernels  39.8 us (26%)
  other arithmetic  5.31 us (4%)
  local copies, waits for them, and re-layouts  2.64 us (2%)
    ppermute x39, waiting for transfers between devices, streamed(): moved = lax.ppermute(join(keys), axis, perms[axis](shift))  58.7 us
    ppermute x39, starting transfers between devices, streamed(): moved = lax.ppermute(join(keys), axis, perms[axis](shift))  42.8 us
    pallas_call x5, Pallas kernels, chunk_call(): pl.pallas_call(functools.partial(chunk_kernel, chunks, blocks, count), ou...  39.8 us
  transfers between devices with their start and end apart: 39, of which 12 were waited for; matrix products, arithmetic and copies ran while one was open for 3% of the time, Pallas kernels for 20%

profile of v3, /device:TPU:0, one launch (start us, length us, event | category | flops | bytes accessed | tf_op | source)
XLA Modules:
  0.0 150.3 jit_solution(12926659748438729202)
XLA Ops:
  0.0 1.3 fusion
  1.4 4.1 %collective-permute-start.3 = (bf16[128,1024]{1,0:T(8,128)(2,1)S(1)}, bf16[128,1024]{1,0:T(8,128)(2,1)S(1)}, u32[]{:S(2)}, u32[]{:S(2)}) collective-permute-start(bf16[128,1024]{1,0:T(8,128)(2,1)S(1)} %get-tuple-element.22.refs_4_), channel_id=1, source_target_pairs={{0,2},{1,3},{2,0},{3,1},{4,6},{5,7},{6,4},{7,5},{8,10},{9,11},{10,... | collective-permute-start | bytes 786440 | tf_op jit(solution)/shard_map/ppermute | solution.py:335
  5.5 1.6 %collective-permute-start.14 = (bf16[128,1024]{1,0:T(8,128)(2,1)S(1)}, bf16[128,1024]{1,0:T(8,128)(2,1)S(1)}, u32[]{:S(2)}, u32[]{:S(2)}) collective-permute-start(bf16[128,1024]{1,0:T(8,128)(2,1)S(1)} %get-tuple-element.21.refs_4_), channel_id=1, source_target_pairs={{0,1},{1,2},{2,3},{3,0},{4,5},{5,6},{6,7},{7,4},{8,9},{9,10},{10,1... | collective-permute-start | bytes 786440 | tf_op jit(solution)/shard_map/ppermute | solution.py:335
  7.1 1.5 %collective-permute-start.10 = (bf16[128,1024]{1,0:T(8,128)(2,1)S(1)}, bf16[128,1024]{1,0:T(8,128)(2,1)S(1)}, u32[]{:S(2)}, u32[]{:S(2)}) collective-permute-start(bf16[128,1024]{1,0:T(8,128)(2,1)S(1)} %get-tuple-element.21.refs_4_), channel_id=1, source_target_pairs={{0,16},{16,0},{1,17},{17,1},{2,18},{18,2},{3,19},{19,3},{4,20},{20... | collective-permute-start | bytes 786440 | tf_op jit(solution)/shard_map/ppermute | solution.py:335
  8.6 2.2 %collective-permute-start.15 = (bf16[128,1024]{1,0:T(8,128)(2,1)S(1)}, bf16[128,1024]{1,0:T(8,128)(2,1)S(1)}, u32[]{:S(2)}, u32[]{:S(2)}) collective-permute-start(bf16[128,1024]{1,0:T(8,128)(2,1)S(1)} %get-tuple-element.23.refs_4_), channel_id=1, source_target_pairs={{0,3},{1,0},{2,1},{3,2},{4,7},{5,4},{6,5},{7,6},{8,11},{9,8},{10,9... | collective-permute-start | bytes 786440 | tf_op jit(solution)/shard_map/ppermute | solution.py:335
  10.8 13.1 %collective-permute-done.3.refs_6_ = bf16[128,1024]{1,0:T(8,128)(2,1)S(1)} collective-permute-done((bf16[128,1024]{1,0:T(8,128)(2,1)S(1)}, bf16[128,1024]{1,0:T(8,128)(2,1)S(1)}, u32[]{:S(2)}, u32[]{:S(2)}) %collective-permute-start.3) | collective-permute-done | bytes 262176 | tf_op jit(solution)/shard_map/ppermute | solution.py:335
  23.9 1.8 %collective-permute-start.4 = (bf16[128,1024]{1,0:T(8,128)(2,1)S(1)}, bf16[128,1024]{1,0:T(8,128)(2,1)}, u32[]{:S(2)}, u32[]{:S(2)}) collective-permute-start(bf16[128,1024]{1,0:T(8,128)(2,1)S(1)} %collective-permute-done.3.refs_6_), channel_id=1, source_target_pairs={{0,8},{4,12},{8,0},{12,4},{1,9},{5,13},{9,1},{13,5},{2,10},{6,14},... | collective-permute-start | bytes 786440 | tf_op jit(solution)/shard_map/ppermute | solution.py:335
  27.2 5.4 %collective-permute-done = f32[1,1152]{1,0:T(1,128)S(1)} collective-permute-done((f32[1,1152]{1,0:T(1,128)S(1)}, f32[1,1152]{1,0:T(1,128)S(1)}, u32[]{:S(2)}, u32[]{:S(2)}) %collective-permute-start) | collective-permute-done | bytes 4640 | tf_op jit(solution)/shard_map/ppermute | solution.py:335
  32.6 4.4 %collective-permute-done.1 = f32[1,1152]{1,0:T(1,128)S(1)} collective-permute-done((f32[1,1152]{1,0:T(1,128)S(1)}, f32[1,1152]{1,0:T(1,128)S(1)}, u32[]{:S(2)}, u32[]{:S(2)}) %collective-permute-start.1) | collective-permute-done | bytes 4640 | tf_op jit(solution)/shard_map/ppermute | solution.py:335
  37.1 3.5 %collective-permute-done.2 = f32[1,1152]{1,0:T(1,128)S(1)} collective-permute-done((f32[1,1152]{1,0:T(1,128)S(1)}, f32[1,1152]{1,0:T(1,128)S(1)}, u32[]{:S(2)}, u32[]{:S(2)}) %collective-permute-start.2) | collective-permute-done | bytes 4640 | tf_op jit(solution)/shard_map/ppermute | solution.py:335
  41.0 1.9 %collective-permute-start.6 = (bf16[128,1024]{1,0:T(8,128)(2,1)S(1)}, bf16[128,1024]{1,0:T(8,128)(2,1)S(1)}, u32[]{:S(2)}, u32[]{:S(2)}) collective-permute-start(bf16[128,1024]{1,0:T(8,128)(2,1)S(1)} %get-tuple-element.23.refs_4_), channel_id=1, source_target_pairs={{0,16},{16,0},{1,17},{17,1},{2,18},{18,2},{3,19},{19,3},{4,20},{20... | collective-permute-start | bytes 786440 | tf_op jit(solution)/shard_map/ppermute | solution.py:335
  44.1 3.0 %collective-permute-done.20.refs_12_ = bf16[128,1024]{1,0:T(8,128)(2,1)S(1)} collective-permute-done((bf16[128,1024]{1,0:T(8,128)(2,1)S(1)}, bf16[128,1024]{1,0:T(8,128)(2,1)S(1)}, u32[]{:S(2)}, u32[]{:S(2)}) %collective-permute-start.20) | collective-permute-done | bytes 262176 | tf_op jit(solution)/shard_map/ppermute | solution.py:335
  47.1 1.8 %collective-permute-start.8 = (bf16[128,1024]{1,0:T(8,128)(2,1)S(1)}, bf16[128,1024]{1,0:T(8,128)(2,1)S(1)}, u32[]{:S(2)}, u32[]{:S(2)}) collective-permute-start(bf16[128,1024]{1,0:T(8,128)(2,1)S(1)} %get-tuple-element.24.refs_4_), channel_id=1, source_target_pairs={{0,3},{1,0},{2,1},{3,2},{4,7},{5,4},{6,5},{7,6},{8,11},{9,8},{10,9... | collective-permute-start | bytes 786440 | tf_op jit(solution)/shard_map/ppermute | solution.py:335
  49.8 2.2 %collective-permute-done.32.refs_5_ = bf16[128,1024]{1,0:T(8,128)(2,1)S(1)} collective-permute-done((bf16[128,1024]{1,0:T(8,128)(2,1)S(1)}, bf16[128,1024]{1,0:T(8,128)(2,1)S(1)}, u32[]{:S(2)}, u32[]{:S(2)}) %collective-permute-start.32) | collective-permute-done | bytes 262176 | tf_op jit(solution)/shard_map/ppermute | solution.py:335
  52.0 1.4 collective-permute-start.28
  53.8 1.6 %collective-permute-start.22 = (bf16[128,1024]{1,0:T(8,128)(2,1)S(1)}, bf16[128,1024]{1,0:T(8,128)(2,1)}, u32[]{:S(2)}, u32[]{:S(2)}) collective-permute-start(bf16[128,1024]{1,0:T(8,128)(2,1)S(1)} %collective-permute-done.15.refs_7_), channel_id=1, source_target_pairs={{0,8},{4,12},{8,0},{12,4},{1,9},{5,13},{9,1},{13,5},{2,10},{6,14},... | collective-permute-start | bytes 786440 | tf_op jit(solution)/shard_map/ppermute | solution.py:335
  57.7 4.3 %collective-permute-start.37 = (bf16[384,1024]{1,0:T(8,128)(2,1)}, bf16[384,1024]{1,0:T(8,128)(2,1)S(1)}, u32[]{:S(2)}, u32[]{:S(2)}) collective-permute-start(bf16[384,1024]{1,0:T(8,128)(2,1)} %pad_maximum_fusion), channel_id=1, source_target_pairs={{0,16},{16,0},{1,17},{17,1},{2,18},{18,2},{3,19},{19,3},{4,20},{20... | collective-permute-start | bytes 2359304 | tf_op jit(solution)/shard_map/ppermute | solution.py:335
  63.3 5.0 %collective-permute-done.28.refs_7_ = bf16[128,1024]{1,0:T(8,128)(2,1)S(1)} collective-permute-done((bf16[128,1024]{1,0:T(8,128)(2,1)S(1)}, bf16[128,1024]{1,0:T(8,128)(2,1)S(1)}, u32[]{:S(2)}, u32[]{:S(2)}) %collective-permute-start.28) | collective-permute-done | bytes 262176 | tf_op jit(solution)/shard_map/ppermute | solution.py:335
  69.0 1.4 collective-permute-start.38
  71.8 11.0 %collective-permute-done.38.refs_5_ = bf16[128,1024]{1,0:T(8,128)(2,1)S(1)} collective-permute-done((bf16[128,1024]{1,0:T(8,128)(2,1)S(1)}, bf16[128,1024]{1,0:T(8,128)(2,1)S(1)}, u32[]{:S(2)}, u32[]{:S(2)}) %collective-permute-start.38) | collective-permute-done | bytes 262176 | tf_op jit(solution)/shard_map/ppermute | solution.py:335
  83.5 1.7 %collective-permute-start.34 = (bf16[128,1024]{1,0:T(8,128)(2,1)S(1)}, bf16[128,1024]{1,0:T(8,128)(2,1)S(1)}, u32[]{:S(2)}, u32[]{:S(2)}) collective-permute-start(bf16[128,1024]{1,0:T(8,128)(2,1)S(1)} %collective-permute-done.32.refs_5_), channel_id=1, source_target_pairs={{0,16},{16,0},{1,17},{17,1},{2,18},{18,2},{3,19},{19,3},{4,20},{20... | collective-permute-start | bytes 786440 | tf_op jit(solution)/shard_map/ppermute | solution.py:335
  85.5 1.7 %collective-permute-start.29 = (bf16[128,1024]{1,0:T(8,128)(2,1)S(1)}, bf16[128,1024]{1,0:T(8,128)(2,1)S(1)}, u32[]{:S(2)}, u32[]{:S(2)}) collective-permute-start(bf16[128,1024]{1,0:T(8,128)(2,1)S(1)} %collective-permute-done.26.refs_5_), channel_id=1, source_target_pairs={{0,16},{16,0},{1,17},{17,1},{2,18},{18,2},{3,19},{19,3},{4,20},{20... | collective-permute-start | bytes 786440 | tf_op jit(solution)/shard_map/ppermute | solution.py:335
  89.4 6.5 %chunk.5 = (f32[4,4,128,1024]{3,2,1,0:T(8,128)}, bf16[512,1024]{1,0:T(8,128)(2,1)S(1)}, bf16[512,3072]{1,0:T(8,128)(2,1)S(1)}) custom-call(s32[3]{0:T(128)S(1)} %pad_add_fusion.2.refs_0_, f32[4,4]{1,0:T(4,128)S(1)} %copy-done, f32[4,1024]{1,0:T(4,128)S(1)} %multiply_exponential_fusion.1.refs_2_, f32[4,3072]{1,0:T(4,128)S(1)} %multiply_exponential_fusion.refs_3_, ...), custom_call_target="tpu_custom_call" | custom-call | flops 2147483648 | bytes 6291456 | tf_op jit(solution)/shard_map/chunk/pallas_call | solution.py:257
  96.0 5.4 %chunk.6.refs_14_ = f32[4,4,128,1024]{3,2,1,0:T(8,128)} custom-call(s32[3]{0:T(128)S(1)} %pad_add_fusion.6.refs_0_, f32[4,4]{1,0:T(4,128)S(1)} %copy-done, f32[4,1024]{1,0:T(4,128)S(1)} %multiply_exponential_fusion.1.refs_2_, f32[4,3072]{1,0:T(4,128)S(1)} %multiply_exponential_fusion.refs_3_, ...), custom_call_target="tpu_custom_call", output_to_operand_aliasing={{}: (8, {})} | custom-call | flops 2147483648 | bytes 6291456 | tf_op jit(solution)/shard_map/chunk/pallas_call | solution.py:257
  101.5 3.2 %collective-permute-start.11 = (bf16[256,1024]{1,0:T(8,128)(2,1)S(1)}, bf16[256,1024]{1,0:T(8,128)(2,1)S(1)}, u32[]{:S(2)}, u32[]{:S(2)}) collective-permute-start(bf16[256,1024]{1,0:T(8,128)(2,1)S(1)} %copy-done.5), channel_id=1, source_target_pairs={{0,3},{1,0},{2,1},{3,2},{4,7},{5,4},{6,5},{7,6},{8,11},{9,8},{10,9... | collective-permute-start | bytes 1572872 | tf_op jit(solution)/shard_map/ppermute | solution.py:335
  104.7 3.8 %collective-permute-start.9 = (bf16[128,1024]{1,0:T(8,128)(2,1)S(1)}, bf16[128,1024]{1,0:T(8,128)(2,1)S(1)}, u32[]{:S(2)}, u32[]{:S(2)}) collective-permute-start(bf16[128,1024]{1,0:T(8,128)(2,1)S(1)} %collective-permute-done.8.refs_7_), channel_id=1, source_target_pairs={{0,3},{1,0},{2,1},{3,2},{4,7},{5,4},{6,5},{7,6},{8,11},{9,8},{10,9... | collective-permute-start | bytes 786440 | tf_op jit(solution)/shard_map/ppermute | solution.py:335
  109.1 2.1 %collective-permute-start.30 = (bf16[128,1024]{1,0:T(8,128)(2,1)S(1)}, bf16[128,1024]{1,0:T(8,128)(2,1)S(1)}, u32[]{:S(2)}, u32[]{:S(2)}) collective-permute-start(bf16[128,1024]{1,0:T(8,128)(2,1)S(1)} %collective-permute-done.27.refs_6_), channel_id=1, source_target_pairs={{0,16},{16,0},{1,17},{17,1},{2,18},{18,2},{3,19},{19,3},{4,20},{20... | collective-permute-start | bytes 786440 | tf_op jit(solution)/shard_map/ppermute | solution.py:335
  111.2 9.3 %chunk.7.refs_14_ = f32[4,4,128,1024]{3,2,1,0:T(8,128)} custom-call(s32[4]{0:T(128)S(1)} %pad_add_fusion.5.refs_0_, f32[4,4]{1,0:T(4,128)S(1)} %copy-done, f32[4,1024]{1,0:T(4,128)S(1)} %multiply_exponential_fusion.1.refs_2_, f32[4,3072]{1,0:T(4,128)S(1)} %multiply_exponential_fusion.refs_3_, ...), custom_call_target="tpu_custom_call", output_to_operand_aliasing={{}: (14, {})} | custom-call | flops 4294967296 | bytes 8388608 | tf_op jit(solution)/shard_map/chunk/pallas_call | solution.py:257
  120.6 9.4 %collective-permute-done.9.refs_6_ = bf16[128,1024]{1,0:T(8,128)(2,1)S(1)} collective-permute-done((bf16[128,1024]{1,0:T(8,128)(2,1)S(1)}, bf16[128,1024]{1,0:T(8,128)(2,1)S(1)}, u32[]{:S(2)}, u32[]{:S(2)}) %collective-permute-start.9) | collective-permute-done | bytes 262176 | tf_op jit(solution)/shard_map/ppermute | solution.py:335
  129.9 1.7 %collective-permute-start.13 = (bf16[128,1024]{1,0:T(8,128)(2,1)S(1)}, bf16[128,1024]{1,0:T(8,128)(2,1)S(1)}, u32[]{:S(2)}, u32[]{:S(2)}) collective-permute-start(bf16[128,1024]{1,0:T(8,128)(2,1)S(1)} %collective-permute-done.9.refs_6_), channel_id=1, source_target_pairs={{0,16},{16,0},{1,17},{17,1},{2,18},{18,2},{3,19},{19,3},{4,20},{20... | collective-permute-start | bytes 786440 | tf_op jit(solution)/shard_map/ppermute | solution.py:335
  131.6 9.3 %chunk.8.refs_12_ = f32[4,4,128,1024]{3,2,1,0:T(8,128)} custom-call(s32[4]{0:T(128)S(1)} %get-tuple-element.26.refs_0_, f32[4,4]{1,0:T(4,128)S(1)} %copy-done, f32[4,1024]{1,0:T(4,128)S(1)} %multiply_exponential_fusion.1.refs_2_, f32[4,3072]{1,0:T(4,128)S(1)} %multiply_exponential_fusion.refs_3_, ...), custom_call_target="tpu_custom_call", output_to_operand_aliasing={{}: (14, {})} | custom-call | flops 4294967296 | bytes 8388608 | tf_op jit(solution)/shard_map/chunk/pallas_call | solution.py:257
  140.9 9.3 %chunk.9 = f32[4,4,128,1024]{3,2,1,0:T(8,128)} custom-call(s32[4]{0:T(128)S(1)} %get-tuple-element.25.refs_0_, f32[4,4]{1,0:T(4,128)S(1)} %copy-done, f32[4,1024]{1,0:T(4,128)S(1)} %multiply_exponential_fusion.1.refs_2_, f32[4,3072]{1,0:T(4,128)S(1)} %multiply_exponential_fusion.refs_3_, ...), custom_call_target="tpu_custom_call", output_to_operand_aliasing={{}: (12, {})} | custom-call | flops 4294967296 | bytes 8388608 | tf_op jit(solution)/shard_map/chunk/pallas_call | solution.py:257
  (83 shorter events, 13.1 us)
Async XLA Ops:
  1.4 22.6 %collective-permute-start.3 = (bf16[128,1024]{1,0:T(8,128)(2,1)S(1)}, bf16[128,1024]{1,0:T(8,128)(2,1)S(1)}, u32[]{:S(2)}, u32[]{:S(2)}) collective-permute-start(bf16[128,1024]{1,0:T(8,128)(2,1)S(1)} %get-tuple-element.22.refs_4_), channel_id=1, source_target_pairs={{0,2},{1,3},{2,0},{3,1},{4,6},{5,7},{6,4},{7,5},{8,10},{9,11},{10,... | collective-permute-start | bytes 786440 | tf_op jit(solution)/shard_map/ppermute | solution.py:335
  5.5 35.4 %collective-permute-start.14 = (bf16[128,1024]{1,0:T(8,128)(2,1)S(1)}, bf16[128,1024]{1,0:T(8,128)(2,1)S(1)}, u32[]{:S(2)}, u32[]{:S(2)}) collective-permute-start(bf16[128,1024]{1,0:T(8,128)(2,1)S(1)} %get-tuple-element.21.refs_4_), channel_id=1, source_target_pairs={{0,1},{1,2},{2,3},{3,0},{4,5},{5,6},{6,7},{7,4},{8,9},{9,10},{10,1... | collective-permute-start | bytes 786440 | tf_op jit(solution)/shard_map/ppermute | solution.py:335
  7.1 33.9 %collective-permute-start.10 = (bf16[128,1024]{1,0:T(8,128)(2,1)S(1)}, bf16[128,1024]{1,0:T(8,128)(2,1)S(1)}, u32[]{:S(2)}, u32[]{:S(2)}) collective-permute-start(bf16[128,1024]{1,0:T(8,128)(2,1)S(1)} %get-tuple-element.21.refs_4_), channel_id=1, source_target_pairs={{0,16},{16,0},{1,17},{17,1},{2,18},{18,2},{3,19},{19,3},{4,20},{20... | collective-permute-start | bytes 786440 | tf_op jit(solution)/shard_map/ppermute | solution.py:335
  8.6 32.3 %collective-permute-start.15 = (bf16[128,1024]{1,0:T(8,128)(2,1)S(1)}, bf16[128,1024]{1,0:T(8,128)(2,1)S(1)}, u32[]{:S(2)}, u32[]{:S(2)}) collective-permute-start(bf16[128,1024]{1,0:T(8,128)(2,1)S(1)} %get-tuple-element.23.refs_4_), channel_id=1, source_target_pairs={{0,3},{1,0},{2,1},{3,2},{4,7},{5,4},{6,5},{7,6},{8,11},{9,8},{10,9... | collective-permute-start | bytes 786440 | tf_op jit(solution)/shard_map/ppermute | solution.py:335
  23.9 19.0 %collective-permute-start.4 = (bf16[128,1024]{1,0:T(8,128)(2,1)S(1)}, bf16[128,1024]{1,0:T(8,128)(2,1)}, u32[]{:S(2)}, u32[]{:S(2)}) collective-permute-start(bf16[128,1024]{1,0:T(8,128)(2,1)S(1)} %collective-permute-done.3.refs_6_), channel_id=1, source_target_pairs={{0,8},{4,12},{8,0},{12,4},{1,9},{5,13},{9,1},{13,5},{2,10},{6,14},... | collective-permute-start | bytes 786440 | tf_op jit(solution)/shard_map/ppermute | solution.py:335
  40.7 6.4 %collective-permute-start.20 = (bf16[128,1024]{1,0:T(8,128)(2,1)S(1)}, bf16[128,1024]{1,0:T(8,128)(2,1)S(1)}, u32[]{:S(2)}, u32[]{:S(2)}) collective-permute-start(bf16[128,1024]{1,0:T(8,128)(2,1)S(1)} %get-tuple-element.24.refs_4_), channel_id=1, source_target_pairs={{0,8},{4,12},{8,0},{12,4},{1,9},{5,13},{9,1},{13,5},{2,10},{6,14},... | collective-permute-start | bytes 786440 | tf_op jit(solution)/shard_map/ppermute | solution.py:335
  40.9 8.0 %collective-permute-start.16 = (bf16[128,1024]{1,0:T(8,128)(2,1)S(1)}, bf16[128,1024]{1,0:T(8,128)(2,1)S(1)}, u32[]{:S(2)}, u32[]{:S(2)}) collective-permute-start(bf16[128,1024]{1,0:T(8,128)(2,1)S(1)} %get-tuple-element.24.refs_4_), channel_id=1, source_target_pairs={{0,4},{4,0},{8,12},{12,8},{1,5},{5,1},{9,13},{13,9},{2,6},{6,2},{1... | collective-permute-start | bytes 786440 | tf_op jit(solution)/shard_map/ppermute | solution.py:335
  40.9 11.1 %collective-permute-start.32 = (bf16[128,1024]{1,0:T(8,128)(2,1)S(1)}, bf16[128,1024]{1,0:T(8,128)(2,1)S(1)}, u32[]{:S(2)}, u32[]{:S(2)}) collective-permute-start(bf16[128,1024]{1,0:T(8,128)(2,1)S(1)} %get-tuple-element.22.refs_4_), channel_id=1, source_target_pairs={{0,1},{1,2},{2,3},{3,0},{4,5},{5,6},{6,7},{7,4},{8,9},{9,10},{10,1... | collective-permute-start | bytes 786440 | tf_op jit(solution)/shard_map/ppermute | solution.py:335
  41.0 12.4 %collective-permute-start.6 = (bf16[128,1024]{1,0:T(8,128)(2,1)S(1)}, bf16[128,1024]{1,0:T(8,128)(2,1)S(1)}, u32[]{:S(2)}, u32[]{:S(2)}) collective-permute-start(bf16[128,1024]{1,0:T(8,128)(2,1)S(1)} %get-tuple-element.23.refs_4_), channel_id=1, source_target_pairs={{0,16},{16,0},{1,17},{17,1},{2,18},{18,2},{3,19},{19,3},{4,20},{20... | collective-permute-start | bytes 786440 | tf_op jit(solution)/shard_map/ppermute | solution.py:335
  42.9 10.9 %collective-permute-start.5 = (bf16[128,1024]{1,0:T(8,128)(2,1)}, bf16[128,1024]{1,0:T(8,128)(2,1)}, u32[]{:S(2)}, u32[]{:S(2)}) collective-permute-start(bf16[128,1024]{1,0:T(8,128)(2,1)} %collective-permute-done.4.refs_14_), channel_id=1, source_target_pairs={{0,4},{4,0},{8,12},{12,8},{1,5},{5,1},{9,13},{13,9},{2,6},{6,2},{1... | collective-permute-start | bytes 786440 | tf_op jit(solution)/shard_map/ppermute | solution.py:335
  47.1 10.6 %collective-permute-start.8 = (bf16[128,1024]{1,0:T(8,128)(2,1)S(1)}, bf16[128,1024]{1,0:T(8,128)(2,1)S(1)}, u32[]{:S(2)}, u32[]{:S(2)}) collective-permute-start(bf16[128,1024]{1,0:T(8,128)(2,1)S(1)} %get-tuple-element.24.refs_4_), channel_id=1, source_target_pairs={{0,3},{1,0},{2,1},{3,2},{4,7},{5,4},{6,5},{7,6},{8,11},{9,8},{10,9... | collective-permute-start | bytes 786440 | tf_op jit(solution)/shard_map/ppermute | solution.py:335
  49.6 13.7 %collective-permute-start.26 = (bf16[128,1024]{1,0:T(8,128)(2,1)S(1)}, bf16[128,1024]{1,0:T(8,128)(2,1)S(1)}, u32[]{:S(2)}, u32[]{:S(2)}) collective-permute-start(bf16[128,1024]{1,0:T(8,128)(2,1)S(1)} %get-tuple-element.24.refs_4_), channel_id=1, source_target_pairs={{0,1},{1,2},{2,3},{3,0},{4,5},{5,6},{6,7},{7,4},{8,9},{9,10},{10,1... | collective-permute-start | bytes 786440 | tf_op jit(solution)/shard_map/ppermute | solution.py:335
  52.0 16.3 %collective-permute-start.28 = (bf16[128,1024]{1,0:T(8,128)(2,1)S(1)}, bf16[128,1024]{1,0:T(8,128)(2,1)S(1)}, u32[]{:S(2)}, u32[]{:S(2)}) collective-permute-start(bf16[128,1024]{1,0:T(8,128)(2,1)S(1)} %get-tuple-element.22.refs_4_), channel_id=1, source_target_pairs={{0,3},{1,0},{2,1},{3,2},{4,7},{5,4},{6,5},{7,6},{8,11},{9,8},{10,9... | collective-permute-start | bytes 786440 | tf_op jit(solution)/shard_map/ppermute | solution.py:335
  53.4 14.9 %collective-permute-start.21 = (bf16[128,1024]{1,0:T(8,128)(2,1)S(1)}, bf16[128,1024]{1,0:T(8,128)(2,1)}, u32[]{:S(2)}, u32[]{:S(2)}) collective-permute-start(bf16[128,1024]{1,0:T(8,128)(2,1)S(1)} %collective-permute-done.14.refs_5_), channel_id=1, source_target_pairs={{0,8},{4,12},{8,0},{12,4},{1,9},{5,13},{9,1},{13,5},{2,10},{6,14},... | collective-permute-start | bytes 786440 | tf_op jit(solution)/shard_map/ppermute | solution.py:335
  53.8 15.0 %collective-permute-start.22 = (bf16[128,1024]{1,0:T(8,128)(2,1)S(1)}, bf16[128,1024]{1,0:T(8,128)(2,1)}, u32[]{:S(2)}, u32[]{:S(2)}) collective-permute-start(bf16[128,1024]{1,0:T(8,128)(2,1)S(1)} %collective-permute-done.15.refs_7_), channel_id=1, source_target_pairs={{0,8},{4,12},{8,0},{12,4},{1,9},{5,13},{9,1},{13,5},{2,10},{6,14},... | collective-permute-start | bytes 786440 | tf_op jit(solution)/shard_map/ppermute | solution.py:335
  57.7 29.6 %collective-permute-start.37 = (bf16[384,1024]{1,0:T(8,128)(2,1)}, bf16[384,1024]{1,0:T(8,128)(2,1)S(1)}, u32[]{:S(2)}, u32[]{:S(2)}) collective-permute-start(bf16[384,1024]{1,0:T(8,128)(2,1)} %pad_maximum_fusion), channel_id=1, source_target_pairs={{0,16},{16,0},{1,17},{17,1},{2,18},{18,2},{3,19},{19,3},{4,20},{20... | collective-permute-start | bytes 2359304 | tf_op jit(solution)/shard_map/ppermute | solution.py:335
  69.0 13.8 %collective-permute-start.38 = (bf16[128,1024]{1,0:T(8,128)(2,1)S(1)}, bf16[128,1024]{1,0:T(8,128)(2,1)S(1)}, u32[]{:S(2)}, u32[]{:S(2)}) collective-permute-start(bf16[128,1024]{1,0:T(8,128)(2,1)S(1)} %collective-permute-done.3.refs_6_), channel_id=1, source_target_pairs={{0,16},{16,0},{1,17},{17,1},{2,18},{18,2},{3,19},{19,3},{4,20},{20... | collective-permute-start | bytes 786440 | tf_op jit(solution)/shard_map/ppermute | solution.py:335
  70.4 13.0 %collective-permute-start.33 = (bf16[128,1024]{1,0:T(8,128)(2,1)S(1)}, bf16[128,1024]{1,0:T(8,128)(2,1)S(1)}, u32[]{:S(2)}, u32[]{:S(2)}) collective-permute-start(bf16[128,1024]{1,0:T(8,128)(2,1)S(1)} %collective-permute-done.15.refs_7_), channel_id=1, source_target_pairs={{0,3},{1,0},{2,1},{3,2},{4,7},{5,4},{6,5},{7,6},{8,11},{9,8},{10,9... | collective-permute-start | bytes 786440 | tf_op jit(solution)/shard_map/ppermute | solution.py:335
  71.2 14.0 %collective-permute-start.24 = (bf16[128,1024]{1,0:T(8,128)(2,1)}, bf16[128,1024]{1,0:T(8,128)(2,1)S(1)}, u32[]{:S(2)}, u32[]{:S(2)}) collective-permute-start(bf16[128,1024]{1,0:T(8,128)(2,1)} %collective-permute-done.21.refs_13_), channel_id=1, source_target_pairs={{0,4},{4,0},{8,12},{12,8},{1,5},{5,1},{9,13},{13,9},{2,6},{6,2},{1... | collective-permute-start | bytes 786440 | tf_op jit(solution)/shard_map/ppermute | solution.py:335
  71.2 14.3 %collective-permute-start.25 = (bf16[128,1024]{1,0:T(8,128)(2,1)}, bf16[128,1024]{1,0:T(8,128)(2,1)S(1)}, u32[]{:S(2)}, u32[]{:S(2)}) collective-permute-start(bf16[128,1024]{1,0:T(8,128)(2,1)} %collective-permute-done.22.refs_15_), channel_id=1, source_target_pairs={{0,4},{4,0},{8,12},{12,8},{1,5},{5,1},{9,13},{13,9},{2,6},{6,2},{1... | collective-permute-start | bytes 786440 | tf_op jit(solution)/shard_map/ppermute | solution.py:335
  82.8 21.9 %collective-permute-start.27 = (bf16[128,1024]{1,0:T(8,128)(2,1)S(1)}, bf16[128,1024]{1,0:T(8,128)(2,1)S(1)}, u32[]{:S(2)}, u32[]{:S(2)}) collective-permute-start(bf16[128,1024]{1,0:T(8,128)(2,1)S(1)} %collective-permute-done.14.refs_5_), channel_id=1, source_target_pairs={{0,1},{1,2},{2,3},{3,0},{4,5},{5,6},{6,7},{7,4},{8,9},{9,10},{10,1... | collective-permute-start | bytes 786440 | tf_op jit(solution)/shard_map/ppermute | solution.py:335
  83.5 18.0 %collective-permute-start.34 = (bf16[128,1024]{1,0:T(8,128)(2,1)S(1)}, bf16[128,1024]{1,0:T(8,128)(2,1)S(1)}, u32[]{:S(2)}, u32[]{:S(2)}) collective-permute-start(bf16[128,1024]{1,0:T(8,128)(2,1)S(1)} %collective-permute-done.32.refs_5_), channel_id=1, source_target_pairs={{0,16},{16,0},{1,17},{17,1},{2,18},{18,2},{3,19},{19,3},{4,20},{20... | collective-permute-start | bytes 786440 | tf_op jit(solution)/shard_map/ppermute | solution.py:335
  85.2 19.5 %collective-permute-start.36 = (bf16[128,1024]{1,0:T(8,128)(2,1)S(1)}, bf16[128,1024]{1,0:T(8,128)(2,1)S(1)}, u32[]{:S(2)}, u32[]{:S(2)}) collective-permute-start(bf16[128,1024]{1,0:T(8,128)(2,1)S(1)} %collective-permute-done.8.refs_7_), channel_id=1, source_target_pairs={{0,16},{16,0},{1,17},{17,1},{2,18},{18,2},{3,19},{19,3},{4,20},{20... | collective-permute-start | bytes 786440 | tf_op jit(solution)/shard_map/ppermute | solution.py:335
  85.5 23.0 %collective-permute-start.29 = (bf16[128,1024]{1,0:T(8,128)(2,1)S(1)}, bf16[128,1024]{1,0:T(8,128)(2,1)S(1)}, u32[]{:S(2)}, u32[]{:S(2)}) collective-permute-start(bf16[128,1024]{1,0:T(8,128)(2,1)S(1)} %collective-permute-done.26.refs_5_), channel_id=1, source_target_pairs={{0,16},{16,0},{1,17},{17,1},{2,18},{18,2},{3,19},{19,3},{4,20},{20... | collective-permute-start | bytes 786440 | tf_op jit(solution)/shard_map/ppermute | solution.py:335
  87.3 21.8 %collective-permute-start.35 = (bf16[128,1024]{1,0:T(8,128)(2,1)S(1)}, bf16[128,1024]{1,0:T(8,128)(2,1)S(1)}, u32[]{:S(2)}, u32[]{:S(2)}) collective-permute-start(bf16[128,1024]{1,0:T(8,128)(2,1)S(1)} %collective-permute-done.33.refs_6_), channel_id=1, source_target_pairs={{0,16},{16,0},{1,17},{17,1},{2,18},{18,2},{3,19},{19,3},{4,20},{20... | collective-permute-start | bytes 786440 | tf_op jit(solution)/shard_map/ppermute | solution.py:335
  101.5 39.4 %collective-permute-start.11 = (bf16[256,1024]{1,0:T(8,128)(2,1)S(1)}, bf16[256,1024]{1,0:T(8,128)(2,1)S(1)}, u32[]{:S(2)}, u32[]{:S(2)}) collective-permute-start(bf16[256,1024]{1,0:T(8,128)(2,1)S(1)} %copy-done.5), channel_id=1, source_target_pairs={{0,3},{1,0},{2,1},{3,2},{4,7},{5,4},{6,5},{7,6},{8,11},{9,8},{10,9... | collective-permute-start | bytes 1572872 | tf_op jit(solution)/shard_map/ppermute | solution.py:335
  104.7 36.2 %collective-permute-start.7 = (bf16[256,1024]{1,0:T(8,128)(2,1)S(1)}, bf16[256,1024]{1,0:T(8,128)(2,1)S(1)}, u32[]{:S(2)}, u32[]{:S(2)}) collective-permute-start(bf16[256,1024]{1,0:T(8,128)(2,1)S(1)} %copy-done.6), channel_id=1, source_target_pairs={{0,1},{1,2},{2,3},{3,0},{4,5},{5,6},{6,7},{7,4},{8,9},{9,10},{10,1... | collective-permute-start | bytes 1572872 | tf_op jit(solution)/shard_map/ppermute | solution.py:335
  104.7 25.2 %collective-permute-start.9 = (bf16[128,1024]{1,0:T(8,128)(2,1)S(1)}, bf16[128,1024]{1,0:T(8,128)(2,1)S(1)}, u32[]{:S(2)}, u32[]{:S(2)}) collective-permute-start(bf16[128,1024]{1,0:T(8,128)(2,1)S(1)} %collective-permute-done.8.refs_7_), channel_id=1, source_target_pairs={{0,3},{1,0},{2,1},{3,2},{4,7},{5,4},{6,5},{7,6},{8,11},{9,8},{10,9... | collective-permute-start | bytes 786440 | tf_op jit(solution)/shard_map/ppermute | solution.py:335
  108.5 11.9 %collective-permute-start.31 = (bf16[128,1024]{1,0:T(8,128)(2,1)S(1)}, bf16[128,1024]{1,0:T(8,128)(2,1)S(1)}, u32[]{:S(2)}, u32[]{:S(2)}) collective-permute-start(bf16[128,1024]{1,0:T(8,128)(2,1)S(1)} %collective-permute-done.28.refs_7_), channel_id=1, source_target_pairs={{0,16},{16,0},{1,17},{17,1},{2,18},{18,2},{3,19},{19,3},{4,20},{20... | collective-permute-start | bytes 786440 | tf_op jit(solution)/shard_map/ppermute | solution.py:335
  109.1 22.5 %collective-permute-start.30 = (bf16[128,1024]{1,0:T(8,128)(2,1)S(1)}, bf16[128,1024]{1,0:T(8,128)(2,1)S(1)}, u32[]{:S(2)}, u32[]{:S(2)}) collective-permute-start(bf16[128,1024]{1,0:T(8,128)(2,1)S(1)} %collective-permute-done.27.refs_6_), channel_id=1, source_target_pairs={{0,16},{16,0},{1,17},{17,1},{2,18},{18,2},{3,19},{19,3},{4,20},{20... | collective-permute-start | bytes 786440 | tf_op jit(solution)/shard_map/ppermute | solution.py:335
  120.5 20.4 %collective-permute-start.12 = (bf16[128,1024]{1,0:T(8,128)(2,1)S(1)}, bf16[128,1024]{1,0:T(8,128)(2,1)S(1)}, u32[]{:S(2)}, u32[]{:S(2)}) collective-permute-start(bf16[128,1024]{1,0:T(8,128)(2,1)S(1)} %get-tuple-element.22.refs_4_), channel_id=1, source_target_pairs={{0,16},{16,0},{1,17},{17,1},{2,18},{18,2},{3,19},{19,3},{4,20},{20... | collective-permute-start | bytes 786440 | tf_op jit(solution)/shard_map/ppermute | solution.py:335
  129.9 11.0 %collective-permute-start.13 = (bf16[128,1024]{1,0:T(8,128)(2,1)S(1)}, bf16[128,1024]{1,0:T(8,128)(2,1)S(1)}, u32[]{:S(2)}, u32[]{:S(2)}) collective-permute-start(bf16[128,1024]{1,0:T(8,128)(2,1)S(1)} %collective-permute-done.9.refs_6_), channel_id=1, source_target_pairs={{0,16},{16,0},{1,17},{17,1},{2,18},{18,2},{3,19},{19,3},{4,20},{20... | collective-permute-start | bytes 786440 | tf_op jit(solution)/shard_map/ppermute | solution.py:335
  (14 other events, 132.9 us)
